TPU v7x, 256 devices: a whole 4x4x8 slice. The times are simulated.
256 devices in a mesh: req: 32 (over x, y, z_lo), tp: 8 (over z_hi, core).
Axes of the slice: x: 4, y: 4, z: 8 (z_hi: 4, z_lo: 2; z = z_hi * 2 + z_lo), core: 2. Of those that a mesh axis runs over, the one named last changes fastest.
Arguments:
- hidden_in: bfloat16 [1024, 24, 3072], P(('req', 'tp')), may hold values from -6 to 6
- norm_gain: float32 [3072], replicated, may hold values from 0.1 to 1.9
- w_q: bfloat16 [3072, 3072], P(None, 'tp'), may hold values from -0.108253175 to 0.108253175
- w_k: bfloat16 [3072, 3072], P(None, 'tp'), may hold values from -3.35584844 to 3.35584844
- w_v: bfloat16 [3072, 3072], P(None, 'tp'), may hold values from -0.109375 to 0.109375
- w_o: bfloat16 [3072, 3072], P('tp'), may hold values from -0.109375 to 0.109375
- lengths: int32 [32, 32], P('req'), may hold values from 1 to 24, 576 in all within a row
- dest: int32 [32, 32, 1], P('req'), may hold values from 0 to 31; in each aligned block of 32 rows (0 to 31, 32 to 63, ..., all dimensions but the last counted through in order) at most 2 rows name the same one
Outputs:
- hidden_out: bfloat16 [1024, 24, 3072], P(('req', 'tp'))
- cache: bfloat16 [2048, 24, 2, 3072], P('req', None, None, 'tp')
Inputs may be any that keep to these rules, and one draw needn't show every extreme that they name: Each replica's lengths sum to 576 and the longest is 24. `dest`: no replica names one destination for more than 2 of its requests, and some replica names one exactly 2 times.
All inputs are finite; a program needn't handle non-finite values.
Results may differ from a plain program's by a relative error of at most 0.015.
Values may be sent and summed in bfloat16 or wider, within the bound.
No kernel may reach another device: no remote copies, remote signals or barrier semaphores. Data moves between devices by JAX's collectives and lax.ppermute only.
A program may use at most 128 MiB of HBM per device.

v0:
```python
import functools

import jax
import jax.numpy as jnp
import numpy as np
from jax import lax
from jax.experimental import pallas as pl
from jax.experimental.pallas import tpu as pltpu
from jax.sharding import Mesh, PartitionSpec as P

HD = 96
CAP = 2
EPS = 1e-05
SLOT = 24
NZ = 8
REQ_REP = 32
REQ_DEV = 4
ROWS = REQ_DEV * SLOT
HALF = ROWS // 2
LANES = 128
VMEM = pl.BlockSpec(memory_space=pltpu.VMEM)
SMEM = pl.BlockSpec(memory_space=pltpu.SMEM)
HBM = pl.BlockSpec(memory_space=pltpu.HBM)


def rope_tables(width):
    half = HD // 2
    pos = np.arange(SLOT, dtype=np.float32)
    inv = (np.float32(10000.0) ** (-(np.arange(half, dtype=np.float32) * 2.0) / HD)).astype(np.float32)
    angle = pos[:, None] * inv[None, :]
    cosine = np.tile(np.cos(angle), (1, 2 * (width // HD)))
    sine = np.tile(np.concatenate([-np.sin(angle), np.sin(angle)], 1), (1, width // HD))
    return jnp.asarray(cosine, jnp.float32), jnp.asarray(sine, jnp.float32)


def rotate(x, cosine, sine):
    rows, width = x.shape
    lane = lax.broadcasted_iota(jnp.int32, x.shape, 1) % HD
    ahead = pltpu.roll(x, width - HD // 2, 1)
    behind = pltpu.roll(x, HD // 2, 1)
    turned = jnp.where(lane < HD // 2, ahead, behind)
    reps = rows // SLOT
    return x * jnp.concatenate([cosine] * reps, 0) + turned * jnp.concatenate([sine] * reps, 0)


def first_request(meta, back, other_core=0):
    chip = (meta[0] - back + NZ) % NZ
    core = meta[1] if not other_core else 1 - meta[1]
    return (chip % 2) * REQ_REP + ((chip // 2) * 2 + core) * REQ_DEV


def load(src, dst, sem):
    pltpu.make_async_copy(src, dst, sem).start()


def landed(dst, sem):
    pltpu.make_async_copy(dst, dst, sem).wait()


def columns(shard, size):
    return pl.ds(pl.multiple_of(shard * size, LANES), size)


def tiled(table, rows):
    return jnp.concatenate([table[...]] * (rows // SLOT), 0)


def score_masks(backs, meta, lens, heads):
    row = lax.broadcasted_iota(jnp.int32, (ROWS, ROWS), 0)
    col = lax.broadcasted_iota(jnp.int32, (ROWS, ROWS), 1)
    causal = (row // SLOT == col // SLOT) & (col <= row)
    which = lax.broadcasted_iota(jnp.int32, (1, ROWS), 1) // SLOT
    masks = []
    for back in backs:
        base = first_request(meta, back)
        limit = jnp.zeros((1, ROWS), jnp.int32)
        for j in range(REQ_DEV):
            limit = jnp.where(which == j, lens[base + j] + j * SLOT, limit)
        mask = jnp.where(causal & (col < limit), 1.0, 0.0)
        masks.append(jnp.concatenate([mask] * heads, 0))
    return masks


def attend_shard(shard, masks, x_scr, k_scr, v_scr, wq_scr, cosine, sine, attn_scr):
    n = len(masks)
    per_dev = wq_scr.shape[-1]
    heads = per_dev // HD
    cols = columns(shard, per_dev)
    head = lax.broadcasted_iota(jnp.int32, (ROWS, per_dev), 1) // HD
    q = jnp.dot(x_scr[: n * ROWS, :], wq_scr[shard], preferred_element_type=jnp.float32)
    q = rotate(q, cosine, sine).astype(jnp.bfloat16).astype(jnp.float32)
    for i in range(n):
        at = slice(i * ROWS, (i + 1) * ROWS)
        qi = q[at]
        stacked = jnp.concatenate([jnp.where(head == h, qi, 0.0) for h in range(heads)], 0)
        scores = lax.dot_general(
            stacked.astype(jnp.bfloat16),
            k_scr[at, cols],
            (((1,), (1,)), ((), ())),
            preferred_element_type=jnp.float32,
        ) * np.float32(1.0 / np.sqrt(np.float32(HD)))
        mask = masks[i] > 0.5
        scores = jnp.where(mask, scores, -1e30)
        peak = jnp.max(scores, -1, keepdims=True)
        expo = jnp.where(mask, jnp.exp(scores - peak), 0.0)
        probs = (expo / jnp.sum(expo, -1, keepdims=True)).astype(jnp.bfloat16)
        y = jnp.dot(probs, v_scr[at, cols], preferred_element_type=jnp.float32)
        attn = jnp.where(head == 0, y[:ROWS], 0.0)
        for h in range(1, heads):
            attn = jnp.where(head == h, y[h * ROWS : (h + 1) * ROWS], attn)
        attn_scr[at, cols] = attn.astype(jnp.bfloat16)


def project(attn_scr, wo_scr, part_scr, outs, sems):
    width = wo_scr.shape[1]
    step = 768

    def body(c, carry):
        cols = columns(c, step)
        y = jnp.dot(attn_scr[...], wo_scr[:, cols], preferred_element_type=jnp.float32)
        part_scr[:, cols] = y.astype(jnp.bfloat16)
        return carry

    lax.fori_loop(0, width // step, body, 0)
    for i, out in enumerate(outs):
        load(part_scr.at[pl.ds(i * HALF, HALF)], out, sems.at[i])


def load_weights(shard, sources, held, sems):
    wk, wv, wq, wo = sources
    wkv_v, wq_v, wo_v = held
    per_dev = wk.shape[1]
    load(wk, wkv_v.at[shard, :, pl.ds(0, per_dev)], sems.at[shard, 0])
    load(wv, wkv_v.at[shard, :, pl.ds(per_dev, per_dev)], sems.at[shard, 1])
    load(wq, wq_v.at[shard], sems.at[shard, 2])
    load(wo, wo_v.at[pl.ds(shard * per_dev, per_dev)], sems.at[shard, 3])


def held_shapes(width, per_dev):
    return [
        pltpu.VMEM((2, width, 2 * per_dev), jnp.bfloat16),
        pltpu.VMEM((2, width, per_dev), jnp.bfloat16),
        pltpu.VMEM((2 * per_dev, width), jnp.bfloat16),
    ]


def pinned(held):
    return [pltpu.with_memory_space_constraint(w, pltpu.VMEM) for w in held]


def kv_kernel(backs, n_att, pieces, fill, *refs):
    refs = list(refs)
    take = lambda count: [refs.pop(0) for _ in range(count)]
    meta, lens, gain, cosine, sine = take(5)
    weights = take(8 if fill else 3)
    chunks = take(pieces)
    wkv_v, wq_v, wo_v = take(3) if fill else weights
    parts = take(2 * n_att)
    wires = take(2)
    g_scr, cos_scr, sin_scr, x_scr, w_scr, wire_scr, small, piece_sem, w_sem, out_sem = take(10)
    if n_att:
        k_scr, v_scr = take(2)
        attn_scr, part_scr, part_sem = take(3)
    per_dev = wq_v.shape[2]
    tiles = per_dev // LANES
    rows = len(backs) * ROWS
    load(gain, g_scr, small.at[0])
    spans, at = [], 0
    for i, ref in enumerate(chunks):
        spans.append(pl.ds(at, ref.shape[0]))
        load(ref, x_scr.at[spans[-1]], piece_sem.at[i])
        at += ref.shape[0]
    load(cosine, cos_scr, small.at[1])
    load(sine, sin_scr, small.at[2])
    if fill:
        load_weights(0, weights[:4], (wkv_v, wq_v, wo_v), w_sem)
        load_weights(1, weights[4:], (wkv_v, wq_v, wo_v), w_sem)
    token = lax.broadcasted_iota(jnp.int32, (SLOT, 1), 0)
    alive = []
    for back in backs:
        base = first_request(meta, back)
        for j in range(REQ_DEV):
            alive.append((token < lens[base + j]).astype(jnp.float32))
    alive = jnp.concatenate(alive, 0)
    masks = score_masks(backs[:n_att], meta, lens, per_dev // HD) if n_att else []
    landed(g_scr, small.at[0])
    for i, span in enumerate(spans):
        landed(x_scr.at[span], piece_sem.at[i])
        xf = x_scr[span, :].astype(jnp.float32)
        mean_sq = jnp.mean(xf * xf, -1, keepdims=True)
        x_scr[span, :] = (xf * lax.rsqrt(mean_sq + EPS) * g_scr[...]).astype(jnp.bfloat16)
    landed(cos_scr, small.at[1])
    landed(sin_scr, small.at[2])

    def body(shard, carry):
        cols = columns(shard, per_dev)
        if fill:
            landed(wkv_v.at[shard, :, pl.ds(0, per_dev)], w_sem.at[shard, 0])
            landed(wkv_v.at[shard, :, pl.ds(per_dev, per_dev)], w_sem.at[shard, 1])
        y = jnp.dot(x_scr[...], wkv_v[shard], preferred_element_type=jnp.float32)
        k = rotate(y[:, :per_dev], cos_scr[...], sin_scr[...]).astype(jnp.bfloat16)
        v = y[:, per_dev:].astype(jnp.bfloat16)
        if n_att:
            k_scr[:, cols] = k[: k_scr.shape[0]]
            v_scr[:, cols] = v[: v_scr.shape[0]]
        for kv, y in enumerate((k, v)):
            y = jnp.where(alive > 0.5, y.astype(jnp.float32), 0.0)
            for t in range(tiles):
                w_scr[pl.ds(2 * t + kv, rows, stride=2 * tiles), :] = y[:, t * LANES : (t + 1) * LANES]
        wire_scr[shard] = w_scr[...].astype(jnp.bfloat16)
        for i, wire in enumerate(wires):

            @pl.when(shard == i)
            def _():
                load(wire_scr.at[i], wire, out_sem.at[i])

        if fill:
            landed(wq_v.at[shard], w_sem.at[shard, 2])
        if n_att:
            attend_shard(shard, masks, x_scr, k_scr, v_scr, wq_v, cos_scr[...], sin_scr[...], attn_scr)
        return carry

    lax.fori_loop(0, 2, body, 0)
    if fill:
        landed(wo_v.at[pl.ds(0, per_dev)], w_sem.at[0, 3])
        landed(wo_v.at[pl.ds(per_dev, per_dev)], w_sem.at[1, 3])
    if n_att:
        project(attn_scr, wo_v, part_scr, parts, part_sem)
        for i, part in enumerate(parts):
            landed(part, part_sem.at[i])
    for i, wire in enumerate(wires):
        landed(wire, out_sem.at[i])


def kv_call(backs, n_att, meta, lens, tables, weights, chunks):
    n = len(backs)
    fill = len(weights) == 8
    width, per_dev = weights[0].shape if fill else weights[1].shape[1:]
    per_req = SLOT * 2 * per_dev // LANES
    bf16 = lambda *shape: jax.ShapeDtypeStruct(shape, jnp.bfloat16)
    scr = lambda *shape: pltpu.VMEM(shape, jnp.bfloat16)
    outs = (held_shapes(width, per_dev) if fill else []) + [bf16(HALF, width)] * (2 * n_att)
    outs += [bf16(n * REQ_DEV * per_req, LANES)] * 2
    dma = pltpu.SemaphoreType.DMA
    scratch = [pltpu.VMEM(y.shape, y.dtype) for y in tables]
    scratch += [
        scr(n * ROWS, width),
        pltpu.VMEM((n * REQ_DEV * per_req, LANES), jnp.float32),
        scr(2, n * REQ_DEV * per_req, LANES),
        dma((3,)),
        dma((len(chunks),)),
        dma((2, 4)),
        dma((2,)),
    ]
    if n_att:
        scratch += [scr(n_att * ROWS, 2 * per_dev)] * 3 + [scr(n_att * ROWS, width), dma((2 * n_att,))]
    res = pl.pallas_call(
        functools.partial(kv_kernel, backs, n_att, len(chunks), fill),
        out_shape=outs,
        in_specs=[SMEM, SMEM] + [HBM] * 3 + ([HBM] * 8 if fill else [VMEM] * 3) + [HBM] * len(chunks),
        out_specs=[VMEM] * (3 * fill) + [HBM] * (len(outs) - 3 * fill),
        scratch_shapes=scratch,
        compiler_params=pltpu.CompilerParams(vmem_limit_bytes=24 << 20),
        cost_estimate=pl.CostEstimate(
            flops=(n + n_att) * ROWS * width * per_dev // 4, bytes_accessed=1 << 18, transcendentals=0
        ),
        name="keys",
    )(meta, lens, *tables, *(weights if fill else pinned(weights)), *chunks)
    wire = [r.reshape(n * REQ_DEV, per_req, LANES) for r in res[-2:]]
    return res[:-2], wire[0], wire[1]


def pack_kernel(order, meta, slots, empty, *refs):
    sources = refs[: len(order)]
    out, *wires, blank, sem, in_sem = refs[len(order) :]
    for i, (src, dst) in enumerate(zip(sources, wires)):
        load(src, dst, in_sem.at[i])
    blank[...] = jnp.zeros_like(blank)
    for s in range(out.shape[0]):

        @pl.when(empty[s] == 1)
        def _():
            pltpu.make_async_copy(blank, out.at[s], sem).start()

    for w, ((backs, other_core), wire) in enumerate(zip(order, wires)):
        landed(wire, in_sem.at[w])
        for i, back in enumerate(backs):
            base = first_request(meta, back, other_core)
            for j in range(REQ_DEV):
                slot = slots[base + j]

                @pl.when(slot >= 0)
                def _():
                    pltpu.make_async_copy(wire.at[i * REQ_DEV + j], out.at[slot], sem).start()

    pltpu.make_async_copy(out, out, sem).wait()


def pack_call(order, meta, slots, empty, wires):
    per_req = wires[0].shape[1]
    rows = empty.shape[0]
    return pl.pallas_call(
        functools.partial(pack_kernel, order),
        out_shape=jax.ShapeDtypeStruct((rows, per_req, LANES), jnp.bfloat16),
        in_specs=[SMEM] * 3 + [HBM] * len(wires),
        out_specs=HBM,
        scratch_shapes=[pltpu.VMEM(w.shape, w.dtype) for w in wires]
        + [pltpu.VMEM((per_req, LANES), jnp.bfloat16), pltpu.SemaphoreType.DMA]
        + [pltpu.SemaphoreType.DMA((len(wires),))],
        compiler_params=pltpu.CompilerParams(vmem_limit_bytes=24 << 20),
        cost_estimate=pl.CostEstimate(flops=0, bytes_accessed=1 << 18, transcendentals=0),
        name="pack",
    )(meta, slots, empty, *wires)


def place_kernel(wire, out, sem):
    copies = []
    for t in range(wire.shape[2]):
        copies.append(
            pltpu.make_async_copy(wire.at[:, :, t], out.at[:, :, :, pl.ds(t * LANES, LANES)], sem.at[t])
        )
        copies[-1].start()
    for copy in copies:
        copy.wait()


def place_call(inbound, per_dev):
    rows = inbound.shape[0]
    tiles = per_dev // LANES
    wire = inbound.reshape(rows, SLOT, tiles, 2, LANES)
    return pl.pallas_call(
        place_kernel,
        out_shape=jax.ShapeDtypeStruct((rows, SLOT, 2, per_dev), jnp.bfloat16),
        in_specs=[VMEM],
        out_specs=HBM,
        scratch_shapes=[pltpu.SemaphoreType.DMA((tiles,))],
        compiler_params=pltpu.CompilerParams(vmem_limit_bytes=8 << 20),
        name="place",
    )(wire)


def swap(x, axis):
    return lax.ppermute(x, axis, [(0, 1), (1, 0)])


def shift(x, by):
    at = lambda z: (z % 2) * (NZ // 2) + z // 2
    return lax.ppermute(x, ("zl", "zh"), [(at(z), at((z + by) % NZ)) for z in range(NZ)])


def on_device(hidden_in, norm_gain, w_q, w_k, w_v, w_o, lengths, dest):
    width = hidden_in.shape[-1]
    per_dev = w_q.shape[1]
    zl, zh, core = lax.axis_index("zl"), lax.axis_index("zh"), lax.axis_index("core")
    meta = jnp.stack([zh * 2 + zl, core]).astype(jnp.int32)
    mine = jnp.concatenate([lengths[0], dest[0, :, 0]])
    theirs = swap(mine, "zl")
    both = jnp.where(zl == 0, jnp.stack([mine, theirs]), jnp.stack([theirs, mine]))
    lens = both[:, :REQ_REP].reshape(-1)
    target = both[:, REQ_REP:]
    same = target[:, :, None] == target[:, None, :]
    earlier = jnp.arange(REQ_REP)[None, :] < jnp.arange(REQ_REP)[:, None]
    rank = jnp.sum((same & earlier[None]).astype(jnp.int32), -1)
    slots = (target // 2) * (2 * CAP) + jnp.arange(2)[:, None] * CAP + rank
    slots = jnp.where(target % 2 == zl, slots, -1).reshape(-1)
    out_rows = lax.axis_size("xy") * 2 * CAP
    empty = 1 - jnp.any(slots[None, :] == jnp.arange(out_rows)[:, None], -1).astype(jnp.int32)

    flat = hidden_in.reshape(ROWS, width)
    bar = lax.optimization_barrier
    tables = (norm_gain.reshape(1, width), *rope_tables(per_dev))
    order, wires = [], []

    def keys(backs, n_att, weights, chunks):
        extra, own, other = kv_call(backs, n_att, meta, lens, tables, weights, chunks)
        order.append((backs, 0))
        wires.append(own)
        order.append((backs, 1))
        wires.append(swap(other, "core"))
        return extra, own

    u1, d1 = shift(flat, 1), shift(flat, -1)
    wk_p, wv_p = swap(w_k, "core"), swap(w_v, "core")
    wk_p, wq_late, wo_late = bar((wk_p, w_q, w_o))
    u1, d1, meta, lens, slots, empty = bar((u1, d1, meta, lens, slots, empty))
    u2, d2 = shift(u1, 1), shift(d1, -1)
    wq_p, wo_p = swap(wq_late, "core"), swap(wo_late, "core")
    weights = (w_k, w_v, w_q, w_o, wk_p, wv_p, wq_p, wo_p)
    extra, done = keys((0, 1, -1), 1, weights, (flat, u1, d1))
    held, part0 = extra[:3], extra[3:]
    u2, d2, done = bar((u2, d2, done))
    wires[0] = done
    u3, d3 = shift(u2, 1), shift(d2, -1)
    (top1, bottom1, top2, bottom2), done = keys((2, -2), 2, held, (u2, d2))
    u3, d3, done = bar((u3, d3, done))
    wires[2] = done
    far = shift(u3[:HALF], 1), shift(d3[HALF:], -1)
    _, done = keys((3, -3), 0, held, (u3, d3))
    wires[4] = done
    near_t, near_b = shift(top1, -2), shift(bottom2, 2)
    (top3, bottom3), _ = keys((4,), 1, held, far)
    passing_t, passing_b = shift(top3, 2), shift(bottom3, -2)
    outbound = pack_call(order, meta, slots, empty, wires)
    inbound = lax.all_to_all(outbound, "xy", split_axis=0, concat_axis=0, tiled=True)
    add = lambda *ys: sum(y.astype(jnp.float32) for y in ys)
    merged_t = shift(add(top2, passing_t).astype(jnp.bfloat16), 2)
    merged_b = shift(add(bottom1, passing_b).astype(jnp.bfloat16), -2)
    top = add(flat[:HALF], part0[0], near_t, merged_t)
    bottom = add(flat[HALF:], part0[1], near_b, merged_b)
    hidden_out = jnp.concatenate([top, bottom]).astype(jnp.bfloat16).reshape(hidden_in.shape)
    return hidden_out, place_call(inbound, per_dev)


def solution(mesh):
    n_req, n_tp = mesh.devices.shape
    fine = Mesh(mesh.devices.reshape(n_req // 2, 2, n_tp // 2, 2), ("xy", "zl", "zh", "core"))
    req, tp = ("xy", "zl"), ("zh", "core")
    placed = (
        P(req + tp, None, None),
        P(),
        P(None, tp),
        P(None, tp),
        P(None, tp),
        P(tp, None),
        P(req, None),
        P(req, None, None),
    )
    return jax.shard_map(
        on_device,
        mesh=fine,
        in_specs=placed,
        out_specs=(P(req + tp, None, None), P(req, None, None, tp)),
        check_vma=False,
    )
```

profile of v0, /device:TPU:32, one launch (start us, length us, event | category | flops | bytes accessed | tf_op | source)
XLA Modules:
  0.0 137.5 jit_solution(13401741903792097466)
XLA Ops:
  0.7 0.5 collective-permute-start.4
  1.2 4.4 %collective-permute-done.3.refs_9_ = bf16[3072,384]{1,0:T(8,128)(2,1)} collective-permute-done((bf16[3072,384]{1,0:T(8,128)(2,1)}, bf16[3072,384]{1,0:T(8,128)(2,1)}, u32[]{:S(2)}, u32[]{:S(2)}) %collective-permute-start.3) | collective-permute-done | bytes 2359328 | tf_op jit(solution)/shard_map/ppermute | solution.py:343
  5.7 0.4 collective-permute-start.6
  6.1 0.7 pad_add_fusion.1
  6.9 1.9 %collective-permute-start.2 = (s32[64]{0:T(128)S(1)}, s32[64]{0:T(128)S(1)}, u32[]{:S(2)}, u32[]{:S(2)}) collective-permute-start(s32[64]{0:T(128)S(1)} %pad_add_fusion.1), channel_id=1, source_target_pairs={{0,8},{8,0},{1,9},{9,1},{2,10},{10,2},{3,11},{11,3},{4,12},{12,4},... | collective-permute-start | bytes 776 | tf_op jit(solution)/shard_map/ppermute | solution.py:343
  8.7 2.0 %collective-permute-start = (bf16[96,3072]{1,0:T(8,128)(2,1)}, bf16[96,3072]{1,0:T(8,128)(2,1)S(1)}, u32[]{:S(2)}, u32[]{:S(2)}) collective-permute-start(bf16[96,3072]{1,0:T(8,128)(2,1)} %bitcast.26), channel_id=1, source_target_pairs={{0,8},{8,2},{2,10},{10,4},{4,12},{12,6},{6,14},{14,0},{1,9},{9,3},... | collective-permute-start | bytes 1769480 | tf_op jit(solution)/shard_map/ppermute | solution.py:348
  10.7 0.7 fusion.8
  11.5 0.7 collective-permute-start.1
  12.9 11.1 %collective-permute-done.refs_14_ = bf16[96,3072]{1,0:T(8,128)(2,1)S(1)} collective-permute-done((bf16[96,3072]{1,0:T(8,128)(2,1)}, bf16[96,3072]{1,0:T(8,128)(2,1)S(1)}, u32[]{:S(2)}, u32[]{:S(2)}) %collective-permute-start) | collective-permute-done | bytes 589856 | tf_op jit(solution)/shard_map/ppermute | solution.py:348
  24.0 2.6 %collective-permute-done.1.refs_15_ = bf16[96,3072]{1,0:T(8,128)(2,1)S(1)} collective-permute-done((bf16[96,3072]{1,0:T(8,128)(2,1)}, bf16[96,3072]{1,0:T(8,128)(2,1)S(1)}, u32[]{:S(2)}, u32[]{:S(2)}) %collective-permute-start.1) | collective-permute-done | bytes 589856 | tf_op jit(solution)/shard_map/ppermute | solution.py:348
  26.6 2.4 %collective-permute-start.7 = (bf16[96,3072]{1,0:T(8,128)(2,1)S(1)}, bf16[96,3072]{1,0:T(8,128)(2,1)S(1)}, u32[]{:S(2)}, u32[]{:S(2)}) collective-permute-start(bf16[96,3072]{1,0:T(8,128)(2,1)S(1)} %collective-permute-done.refs_14_), channel_id=1, source_target_pairs={{0,8},{8,2},{2,10},{10,4},{4,12},{12,6},{6,14},{14,0},{1,9},{9,3},... | collective-permute-start | bytes 1769480 | tf_op jit(solution)/shard_map/ppermute | solution.py:348
  29.0 1.7 %copy-done = bf16[3072,384]{1,0:T(8,128)(2,1)S(1)} copy-done((bf16[3072,384]{1,0:T(8,128)(2,1)S(1)}, bf16[3072,384]{1,0:T(8,128)(2,1)}, u32[]{:S(2)}) %copy-start) | copy-done | bytes 2359320
  30.7 1.7 %copy-done.1 = bf16[3072,384]{1,0:T(8,128)(2,1)S(1)} copy-done((bf16[3072,384]{1,0:T(8,128)(2,1)S(1)}, bf16[3072,384]{1,0:T(8,128)(2,1)}, u32[]{:S(2)}) %copy-start.1) | copy-done | bytes 2359320
  32.4 1.7 %copy-done.2 = bf16[3072,384]{1,0:T(8,128)(2,1)S(1)} copy-done((bf16[3072,384]{1,0:T(8,128)(2,1)S(1)}, bf16[3072,384]{1,0:T(8,128)(2,1)}, u32[]{:S(2)}) %copy-start.2) | copy-done | bytes 2359320
  34.0 1.1 copy-done.3
  35.1 0.8 copy-done.4
  35.8 0.8 copy-done.5
  36.6 0.7 copy-done.6
  37.3 12.1 %keys.4 = (bf16[2,3072,768]{2,1,0:T(8,128)(2,1)S(1)}, bf16[2,3072,384]{2,1,0:T(8,128)(2,1)S(1)}, bf16[768,3072]{1,0:T(8,128)(2,1)S(1)}, bf16[48,3072]{1,0:T(8,12...) custom-call(s32[2]{0:T(128)S(1)} %pad_add_fusion.refs_0_.meta, ...), custom_call_target="tpu_custom_call" | custom-call | flops 113246208 | bytes 262144 | tf_op jit(solution)/shard_map/keys/pallas_call | solution.py:257
  49.5 3.0 %collective-permute-start.10 = (bf16[96,3072]{1,0:T(8,128)(2,1)S(1)}, bf16[96,3072]{1,0:T(8,128)(2,1)S(1)}, u32[]{:S(2)}, u32[]{:S(2)}) collective-permute-start(bf16[96,3072]{1,0:T(8,128)(2,1)S(1)} %collective-permute-done.7.refs_8_), channel_id=1, source_target_pairs={{0,8},{8,2},{2,10},{10,4},{4,12},{12,6},{6,14},{14,0},{1,9},{9,3},... | collective-permute-start | bytes 1769480 | tf_op jit(solution)/shard_map/ppermute | solution.py:348
  52.9 11.6 %keys.5 = (bf16[48,3072]{1,0:T(8,128)(2,1)}, bf16[48,3072]{1,0:T(8,128)(2,1)S(1)}, bf16[48,3072]{1,0:T(8,128)(2,1)S(1)}, bf16[48,3072]{1,0:T(8,128)(2,1)}, bf16[...) custom-call(s32[2]{0:T(128)S(1)} %pad_add_fusion.refs_0_.meta, s32[64]{0:T(128)S(1)} %reshape.73.refs_1_, ...), custom_call_target="tpu_custom_call" | custom-call | flops 113246208 | bytes 262144 | tf_op jit(solution)/shard_map/keys/pallas_call | solution.py:257
  64.4 1.4 %collective-permute-done.11.refs_9_ = bf16[96,3072]{1,0:T(8,128)(2,1)S(1)} collective-permute-done((bf16[96,3072]{1,0:T(8,128)(2,1)S(1)}, bf16[96,3072]{1,0:T(8,128)(2,1)S(1)}, u32[]{:S(2)}, u32[]{:S(2)}) %collective-permute-start.11) | collective-permute-done | bytes 589856 | tf_op jit(solution)/shard_map/ppermute | solution.py:348
  65.9 1.8 %collective-permute-start.12 = (bf16[48,3072]{1,0:T(8,128)(2,1)S(1)}, bf16[48,3072]{1,0:T(8,128)(2,1)S(1)}, u32[]{:S(2)}, u32[]{:S(2)}) collective-permute-start(bf16[48,3072]{1,0:T(8,128)(2,1)S(1)} %slice.23), channel_id=1, source_target_pairs={{0,8},{8,2},{2,10},{10,4},{4,12},{12,6},{6,14},{14,0},{1,9},{9,3},... | collective-permute-start | bytes 884744 | tf_op jit(solution)/shard_map/ppermute | solution.py:348
  67.7 0.4 collective-permute-start.13
  68.1 0.5 collective-permute-start.19
  68.6 4.4 %keys.7 = (bf16[1152,128]{1,0:T(8,128)(2,1)S(1)}, bf16[1152,128]{1,0:T(8,128)(2,1)S(1)}) custom-call(s32[2]{0:T(128)S(1)} %pad_add_fusion.refs_0_.meta, s32[64]{0:T(128)S(1)} %reshape.73.refs_1_, f32[1,3072]{1,0:T(1,128)S(1)} %bitcast.34, f32[24,384]{1,0:T(8,128)S(1)} %copy-done.4, f32[24,384]{1,0:T(8,128)S(1)} %copy-done.5, ...), custom_call_target="tpu_custom_call" | custom-call | flops 56623104 | bytes 262144 | tf_op jit(solution)/shard_map/keys/pallas_call | solution.py:257
  73.1 2.1 %collective-permute-done.13.refs_9_ = bf16[48,3072]{1,0:T(8,128)(2,1)S(1)} collective-permute-done((bf16[48,3072]{1,0:T(8,128)(2,1)S(1)}, bf16[48,3072]{1,0:T(8,128)(2,1)S(1)}, u32[]{:S(2)}, u32[]{:S(2)}) %collective-permute-start.13) | collective-permute-done | bytes 294944 | tf_op jit(solution)/shard_map/ppermute | solution.py:348
  75.2 8.8 %keys.6 = (bf16[48,3072]{1,0:T(8,128)(2,1)}, bf16[48,3072]{1,0:T(8,128)(2,1)}, bf16[576,128]{1,0:T(8,128)(2,1)S(1)}, bf16[576,128]{1,0:T(8,128)(2,1)S(1)}) custom-call(s32[2]{0:T(128)S(1)} %pad_add_fusion.refs_0_.meta, s32[64]{0:T(128)S(1)} %reshape.73.refs_1_, f32[1,3072]{1,0:T(1,128)S(1)} %bitcast.35, f32[24,384]{1,0:T(8,128)S(1)} %copy-done.4, ...), custom_call_target="tpu_custom_call" | custom-call | flops 56623104 | bytes 262144 | tf_op jit(solution)/shard_map/keys/pallas_call | solution.py:257
  84.1 3.2 %collective-permute-start.14 = (bf16[48,3072]{1,0:T(8,128)(2,1)}, bf16[48,3072]{1,0:T(8,128)(2,1)}, u32[]{:S(2)}, u32[]{:S(2)}) collective-permute-start(bf16[48,3072]{1,0:T(8,128)(2,1)} %get-tuple-element.55), channel_id=1, source_target_pairs={{0,2},{8,10},{2,4},{10,12},{4,6},{12,14},{6,0},{14,8},{1,3},{9,11}... | collective-permute-start | bytes 884744 | tf_op jit(solution)/shard_map/ppermute | solution.py:348
  87.3 0.9 fusion.7
  88.2 1.2 collective-permute-start.9
  89.4 1.7 %collective-permute-start.16 = (bf16[48,3072]{1,0:T(8,128)(2,1)}, bf16[48,3072]{1,0:T(8,128)(2,1)}, u32[]{:S(2)}, u32[]{:S(2)}) collective-permute-start(bf16[48,3072]{1,0:T(8,128)(2,1)} %get-tuple-element.57), channel_id=1, source_target_pairs={{0,2},{8,10},{2,4},{10,12},{4,6},{12,14},{6,0},{14,8},{1,3},{9,11}... | collective-permute-start | bytes 884744 | tf_op jit(solution)/shard_map/ppermute | solution.py:348
  91.2 2.4 %collective-permute-start.17 = (bf16[48,3072]{1,0:T(8,128)(2,1)}, bf16[48,3072]{1,0:T(8,128)(2,1)}, u32[]{:S(2)}, u32[]{:S(2)}) collective-permute-start(bf16[48,3072]{1,0:T(8,128)(2,1)} %get-tuple-element.59), channel_id=1, source_target_pairs={{0,6},{8,14},{2,0},{10,8},{4,2},{12,10},{6,4},{14,12},{1,7},{9,15}... | collective-permute-start | bytes 884744 | tf_op jit(solution)/shard_map/ppermute | solution.py:348
  93.6 3.1 %pack.1 = bf16[64,144,128]{2,1,0:T(8,128)(2,1)} custom-call(s32[2]{0:T(128)S(1)} %pad_add_fusion.refs_0_.meta, s32[64]{0:T(128)S(1)} %reshape.74.slots, s32[64]{0:T(128)S(1)} %convert_subtract_fusion.empty, bf16[12,144,128]{2,1,0:T(8,128)(2,1)S(1)} %bitcast.29, bf16[12,144,128]{2,1,0:T(8,128)(2,1)S(1)} %collective-permute-done.19.refs_1_, ...), custom_call_target="tpu_custom_call" | custom-call | bytes 262144 | tf_op jit(solution)/shard_map/pack/pallas_call | solution.py:302
  96.7 7.0 %all-to-all-start = ((bf16[64,144,128]{2,1,0:T(8,128)(2,1)}), bf16[64,144,128]{2,1,0:T(8,128)(2,1)S(1)}, u32[]{:S(2)}, u32[]{:S(2)}) async-start(bf16[64,144,128]{2,1,0:T(8,128)(2,1)} %pack.1), calls=%async_computation | async-start | bytes 4718592 | tf_op jit(solution)/shard_map/all_to_all | solution.py:404
  103.7 3.7 %collective-permute-done.14 = bf16[48,3072]{1,0:T(8,128)(2,1)} collective-permute-done((bf16[48,3072]{1,0:T(8,128)(2,1)}, bf16[48,3072]{1,0:T(8,128)(2,1)}, u32[]{:S(2)}, u32[]{:S(2)}) %collective-permute-start.14) | collective-permute-done | bytes 294944 | tf_op jit(solution)/shard_map/ppermute | solution.py:348
  107.5 1.0 add_convert_fusion.1
  108.5 2.0 %collective-permute-start.15 = (bf16[48,3072]{1,0:T(8,128)(2,1)S(1)}, bf16[48,3072]{1,0:T(8,128)(2,1)S(1)}, u32[]{:S(2)}, u32[]{:S(2)}) collective-permute-start(bf16[48,3072]{1,0:T(8,128)(2,1)S(1)} %add_convert_fusion.1), channel_id=1, source_target_pairs={{0,2},{8,10},{2,4},{10,12},{4,6},{12,14},{6,0},{14,8},{1,3},{9,11}... | collective-permute-start | bytes 884744 | tf_op jit(solution)/shard_map/ppermute | solution.py:348
  110.5 6.2 %collective-permute-done.17 = bf16[48,3072]{1,0:T(8,128)(2,1)} collective-permute-done((bf16[48,3072]{1,0:T(8,128)(2,1)}, bf16[48,3072]{1,0:T(8,128)(2,1)}, u32[]{:S(2)}, u32[]{:S(2)}) %collective-permute-start.17) | collective-permute-done | bytes 294944 | tf_op jit(solution)/shard_map/ppermute | solution.py:348
  116.8 1.0 add_convert_fusion
  117.8 2.8 %collective-permute-start.18 = (bf16[48,3072]{1,0:T(8,128)(2,1)S(1)}, bf16[48,3072]{1,0:T(8,128)(2,1)S(1)}, u32[]{:S(2)}, u32[]{:S(2)}) collective-permute-start(bf16[48,3072]{1,0:T(8,128)(2,1)S(1)} %add_convert_fusion), channel_id=1, source_target_pairs={{0,6},{8,14},{2,0},{10,8},{4,2},{12,10},{6,4},{14,12},{1,7},{9,15}... | collective-permute-start | bytes 884744 | tf_op jit(solution)/shard_map/ppermute | solution.py:348
  120.7 6.8 %collective-permute-done.15 = bf16[48,3072]{1,0:T(8,128)(2,1)S(1)} collective-permute-done((bf16[48,3072]{1,0:T(8,128)(2,1)S(1)}, bf16[48,3072]{1,0:T(8,128)(2,1)S(1)}, u32[]{:S(2)}, u32[]{:S(2)}) %collective-permute-start.15) | collective-permute-done | bytes 294944 | tf_op jit(solution)/shard_map/ppermute | solution.py:348
  127.4 1.2 fusion.5
  128.6 4.1 %collective-permute-done.18 = bf16[48,3072]{1,0:T(8,128)(2,1)S(1)} collective-permute-done((bf16[48,3072]{1,0:T(8,128)(2,1)S(1)}, bf16[48,3072]{1,0:T(8,128)(2,1)S(1)}, u32[]{:S(2)}, u32[]{:S(2)}) %collective-permute-start.18) | collective-permute-done | bytes 294944 | tf_op jit(solution)/shard_map/ppermute | solution.py:348
  132.7 1.1 fusion.2
  133.8 0.9 pad_maximum_fusion
  134.7 1.2 all-to-all-done
  135.9 1.4 %place.1 = bf16[64,24,2,384]{3,2,1,0:T(2,128)(2,1)} custom-call(bf16[64,24,3,2,128]{4,3,2,1,0:T(2,128)(2,1)S(1)} %bitcast.25), custom_call_target="tpu_custom_call" | custom-call | tf_op jit(solution)/shard_map/place/pallas_call | solution.py:331
  (43 shorter events, 1.6 us)
Async XLA Ops:
  0.6 5.0 %collective-permute-start.3 = (bf16[3072,384]{1,0:T(8,128)(2,1)}, bf16[3072,384]{1,0:T(8,128)(2,1)}, u32[]{:S(2)}, u32[]{:S(2)}) collective-permute-start(bf16[3072,384]{1,0:T(8,128)(2,1)} %refs_5_.1), channel_id=1, source_target_pairs={{0,1},{1,0},{2,3},{3,2},{4,5},{5,4},{6,7},{7,6},{8,9},{9,8},{10,11... | collective-permute-start | bytes 7077896 | tf_op jit(solution)/shard_map/ppermute | solution.py:343
  0.7 28.3 %collective-permute-start.4 = (bf16[3072,384]{1,0:T(8,128)(2,1)}, bf16[3072,384]{1,0:T(8,128)(2,1)}, u32[]{:S(2)}, u32[]{:S(2)}) collective-permute-start(bf16[3072,384]{1,0:T(8,128)(2,1)} %refs_6_.1), channel_id=1, source_target_pairs={{0,1},{1,0},{2,3},{3,2},{4,5},{5,4},{6,7},{7,6},{8,9},{9,8},{10,11... | collective-permute-start | bytes 7077896 | tf_op jit(solution)/shard_map/ppermute | solution.py:343
  5.6 23.4 %collective-permute-start.5 = (bf16[3072,384]{1,0:T(8,128)(2,1)}, bf16[3072,384]{1,0:T(8,128)(2,1)}, u32[]{:S(2)}, u32[]{:S(2)}) collective-permute-start(bf16[3072,384]{1,0:T(8,128)(2,1)} %refs_7_.1), channel_id=1, source_target_pairs={{0,1},{1,0},{2,3},{3,2},{4,5},{5,4},{6,7},{7,6},{8,9},{9,8},{10,11... | collective-permute-start | bytes 7077896 | tf_op jit(solution)/shard_map/ppermute | solution.py:343
  5.7 23.3 %collective-permute-start.6 = (bf16[384,3072]{1,0:T(8,128)(2,1)}, bf16[384,3072]{1,0:T(8,128)(2,1)}, u32[]{:S(2)}, u32[]{:S(2)}) collective-permute-start(bf16[384,3072]{1,0:T(8,128)(2,1)} %refs_8_.1), channel_id=1, source_target_pairs={{0,1},{1,0},{2,3},{3,2},{4,5},{5,4},{6,7},{7,6},{8,9},{9,8},{10,11... | collective-permute-start | bytes 7077896 | tf_op jit(solution)/shard_map/ppermute | solution.py:343
  6.9 4.7 %collective-permute-start.2 = (s32[64]{0:T(128)S(1)}, s32[64]{0:T(128)S(1)}, u32[]{:S(2)}, u32[]{:S(2)}) collective-permute-start(s32[64]{0:T(128)S(1)} %pad_add_fusion.1), channel_id=1, source_target_pairs={{0,8},{8,0},{1,9},{9,1},{2,10},{10,2},{3,11},{11,3},{4,12},{12,4},... | collective-permute-start | bytes 776 | tf_op jit(solution)/shard_map/ppermute | solution.py:343
  8.7 15.3 %collective-permute-start = (bf16[96,3072]{1,0:T(8,128)(2,1)}, bf16[96,3072]{1,0:T(8,128)(2,1)S(1)}, u32[]{:S(2)}, u32[]{:S(2)}) collective-permute-start(bf16[96,3072]{1,0:T(8,128)(2,1)} %bitcast.26), channel_id=1, source_target_pairs={{0,8},{8,2},{2,10},{10,4},{4,12},{12,6},{6,14},{14,0},{1,9},{9,3},... | collective-permute-start | bytes 1769480 | tf_op jit(solution)/shard_map/ppermute | solution.py:348
  11.5 15.0 %collective-permute-start.1 = (bf16[96,3072]{1,0:T(8,128)(2,1)}, bf16[96,3072]{1,0:T(8,128)(2,1)S(1)}, u32[]{:S(2)}, u32[]{:S(2)}) collective-permute-start(bf16[96,3072]{1,0:T(8,128)(2,1)} %bitcast.27), channel_id=1, source_target_pairs={{0,14},{8,0},{2,8},{10,2},{4,10},{12,4},{6,12},{14,6},{1,15},{9,1}... | collective-permute-start | bytes 1769480 | tf_op jit(solution)/shard_map/ppermute | solution.py:348
  26.6 22.9 %collective-permute-start.7 = (bf16[96,3072]{1,0:T(8,128)(2,1)S(1)}, bf16[96,3072]{1,0:T(8,128)(2,1)S(1)}, u32[]{:S(2)}, u32[]{:S(2)}) collective-permute-start(bf16[96,3072]{1,0:T(8,128)(2,1)S(1)} %collective-permute-done.refs_14_), channel_id=1, source_target_pairs={{0,8},{8,2},{2,10},{10,4},{4,12},{12,6},{6,14},{14,0},{1,9},{9,3},... | collective-permute-start | bytes 1769480 | tf_op jit(solution)/shard_map/ppermute | solution.py:348
  29.0 20.5 %collective-permute-start.8 = (bf16[96,3072]{1,0:T(8,128)(2,1)S(1)}, bf16[96,3072]{1,0:T(8,128)(2,1)S(1)}, u32[]{:S(2)}, u32[]{:S(2)}) collective-permute-start(bf16[96,3072]{1,0:T(8,128)(2,1)S(1)} %collective-permute-done.1.refs_15_), channel_id=1, source_target_pairs={{0,14},{8,0},{2,8},{10,2},{4,10},{12,4},{6,12},{14,6},{1,15},{9,1}... | collective-permute-start | bytes 1769480 | tf_op jit(solution)/shard_map/ppermute | solution.py:348
  29.0 1.7 %copy-start = (bf16[3072,384]{1,0:T(8,128)(2,1)S(1)}, bf16[3072,384]{1,0:T(8,128)(2,1)}, u32[]{:S(2)}) copy-start(bf16[3072,384]{1,0:T(8,128)(2,1)} %refs_5_.1) | copy-start | bytes 7077892
  30.7 1.7 %copy-start.1 = (bf16[3072,384]{1,0:T(8,128)(2,1)S(1)}, bf16[3072,384]{1,0:T(8,128)(2,1)}, u32[]{:S(2)}) copy-start(bf16[3072,384]{1,0:T(8,128)(2,1)} %refs_6_.1) | copy-start | bytes 7077892
  32.3 1.7 %copy-start.2 = (bf16[3072,384]{1,0:T(8,128)(2,1)S(1)}, bf16[3072,384]{1,0:T(8,128)(2,1)}, u32[]{:S(2)}) copy-start(bf16[3072,384]{1,0:T(8,128)(2,1)} %refs_7_.1) | copy-start | bytes 7077892
  34.0 1.1 copy-start.3
  35.1 0.8 copy-start.4
  35.8 0.8 copy-start.5
  36.6 0.7 copy-start.6
  49.5 14.9 %collective-permute-start.10 = (bf16[96,3072]{1,0:T(8,128)(2,1)S(1)}, bf16[96,3072]{1,0:T(8,128)(2,1)S(1)}, u32[]{:S(2)}, u32[]{:S(2)}) collective-permute-start(bf16[96,3072]{1,0:T(8,128)(2,1)S(1)} %collective-permute-done.7.refs_8_), channel_id=1, source_target_pairs={{0,8},{8,2},{2,10},{10,4},{4,12},{12,6},{6,14},{14,0},{1,9},{9,3},... | collective-permute-start | bytes 1769480 | tf_op jit(solution)/shard_map/ppermute | solution.py:348
  52.5 13.3 %collective-permute-start.11 = (bf16[96,3072]{1,0:T(8,128)(2,1)S(1)}, bf16[96,3072]{1,0:T(8,128)(2,1)S(1)}, u32[]{:S(2)}, u32[]{:S(2)}) collective-permute-start(bf16[96,3072]{1,0:T(8,128)(2,1)S(1)} %collective-permute-done.8.refs_9_), channel_id=1, source_target_pairs={{0,14},{8,0},{2,8},{10,2},{4,10},{12,4},{6,12},{14,6},{1,15},{9,1}... | collective-permute-start | bytes 1769480 | tf_op jit(solution)/shard_map/ppermute | solution.py:348
  65.9 7.2 %collective-permute-start.12 = (bf16[48,3072]{1,0:T(8,128)(2,1)S(1)}, bf16[48,3072]{1,0:T(8,128)(2,1)S(1)}, u32[]{:S(2)}, u32[]{:S(2)}) collective-permute-start(bf16[48,3072]{1,0:T(8,128)(2,1)S(1)} %slice.23), channel_id=1, source_target_pairs={{0,8},{8,2},{2,10},{10,4},{4,12},{12,6},{6,14},{14,0},{1,9},{9,3},... | collective-permute-start | bytes 884744 | tf_op jit(solution)/shard_map/ppermute | solution.py:348
  67.7 7.5 %collective-permute-start.13 = (bf16[48,3072]{1,0:T(8,128)(2,1)S(1)}, bf16[48,3072]{1,0:T(8,128)(2,1)S(1)}, u32[]{:S(2)}, u32[]{:S(2)}) collective-permute-start(bf16[48,3072]{1,0:T(8,128)(2,1)S(1)} %slice.24), channel_id=1, source_target_pairs={{0,14},{8,0},{2,8},{10,2},{4,10},{12,4},{6,12},{14,6},{1,15},{9,1}... | collective-permute-start | bytes 884744 | tf_op jit(solution)/shard_map/ppermute | solution.py:348
  68.1 20.1 %collective-permute-start.20 = (bf16[8,144,128]{2,1,0:T(8,128)(2,1)S(1)}, bf16[8,144,128]{2,1,0:T(8,128)(2,1)S(1)}, u32[]{:S(2)}, u32[]{:S(2)}) collective-permute-start(bf16[8,144,128]{2,1,0:T(8,128)(2,1)S(1)} %bitcast.38), channel_id=1, source_target_pairs={{0,1},{1,0},{2,3},{3,2},{4,5},{5,4},{6,7},{7,6},{8,9},{9,8},{10,11... | collective-permute-start | bytes 884744 | tf_op jit(solution)/shard_map/ppermute | solution.py:343
  68.1 21.3 %collective-permute-start.19 = (bf16[12,144,128]{2,1,0:T(8,128)(2,1)S(1)}, bf16[12,144,128]{2,1,0:T(8,128)(2,1)S(1)}, u32[]{:S(2)}, u32[]{:S(2)}) collective-permute-start(bf16[12,144,128]{2,1,0:T(8,128)(2,1)S(1)} %bitcast.37), channel_id=1, source_target_pairs={{0,1},{1,0},{2,3},{3,2},{4,5},{5,4},{6,7},{7,6},{8,9},{9,8},{10,11... | collective-permute-start | bytes 1327112 | tf_op jit(solution)/shard_map/ppermute | solution.py:343
  73.0 18.2 %collective-permute-start.21 = (bf16[8,144,128]{2,1,0:T(8,128)(2,1)S(1)}, bf16[8,144,128]{2,1,0:T(8,128)(2,1)S(1)}, u32[]{:S(2)}, u32[]{:S(2)}) collective-permute-start(bf16[8,144,128]{2,1,0:T(8,128)(2,1)S(1)} %bitcast.39), channel_id=1, source_target_pairs={{0,1},{1,0},{2,3},{3,2},{4,5},{5,4},{6,7},{7,6},{8,9},{9,8},{10,11... | collective-permute-start | bytes 884744 | tf_op jit(solution)/shard_map/ppermute | solution.py:343
  84.0 9.6 %collective-permute-start.22 = (bf16[4,144,128]{2,1,0:T(8,128)(2,1)S(1)}, bf16[4,144,128]{2,1,0:T(8,128)(2,1)S(1)}, u32[]{:S(2)}, u32[]{:S(2)}) collective-permute-start(bf16[4,144,128]{2,1,0:T(8,128)(2,1)S(1)} %bitcast.40), channel_id=1, source_target_pairs={{0,1},{1,0},{2,3},{3,2},{4,5},{5,4},{6,7},{7,6},{8,9},{9,8},{10,11... | collective-permute-start | bytes 442376 | tf_op jit(solution)/shard_map/ppermute | solution.py:343
  84.1 23.4 %collective-permute-start.14 = (bf16[48,3072]{1,0:T(8,128)(2,1)}, bf16[48,3072]{1,0:T(8,128)(2,1)}, u32[]{:S(2)}, u32[]{:S(2)}) collective-permute-start(bf16[48,3072]{1,0:T(8,128)(2,1)} %get-tuple-element.55), channel_id=1, source_target_pairs={{0,2},{8,10},{2,4},{10,12},{4,6},{12,14},{6,0},{14,8},{1,3},{9,11}... | collective-permute-start | bytes 884744 | tf_op jit(solution)/shard_map/ppermute | solution.py:348
  88.2 32.4 %collective-permute-start.9 = (bf16[48,3072]{1,0:T(8,128)(2,1)}, bf16[48,3072]{1,0:T(8,128)(2,1)}, u32[]{:S(2)}, u32[]{:S(2)}) collective-permute-start(bf16[48,3072]{1,0:T(8,128)(2,1)} %get-tuple-element.50), channel_id=1, source_target_pairs={{0,6},{8,14},{2,0},{10,8},{4,2},{12,10},{6,4},{14,12},{1,7},{9,15}... | collective-permute-start | bytes 884744 | tf_op jit(solution)/shard_map/ppermute | solution.py:348
  89.4 39.2 %collective-permute-start.16 = (bf16[48,3072]{1,0:T(8,128)(2,1)}, bf16[48,3072]{1,0:T(8,128)(2,1)}, u32[]{:S(2)}, u32[]{:S(2)}) collective-permute-start(bf16[48,3072]{1,0:T(8,128)(2,1)} %get-tuple-element.57), channel_id=1, source_target_pairs={{0,2},{8,10},{2,4},{10,12},{4,6},{12,14},{6,0},{14,8},{1,3},{9,11}... | collective-permute-start | bytes 884744 | tf_op jit(solution)/shard_map/ppermute | solution.py:348
  91.2 25.6 %collective-permute-start.17 = (bf16[48,3072]{1,0:T(8,128)(2,1)}, bf16[48,3072]{1,0:T(8,128)(2,1)}, u32[]{:S(2)}, u32[]{:S(2)}) collective-permute-start(bf16[48,3072]{1,0:T(8,128)(2,1)} %get-tuple-element.59), channel_id=1, source_target_pairs={{0,6},{8,14},{2,0},{10,8},{4,2},{12,10},{6,4},{14,12},{1,7},{9,15}... | collective-permute-start | bytes 884744 | tf_op jit(solution)/shard_map/ppermute | solution.py:348
  96.7 39.2 %all-to-all-start = ((bf16[64,144,128]{2,1,0:T(8,128)(2,1)}), bf16[64,144,128]{2,1,0:T(8,128)(2,1)S(1)}, u32[]{:S(2)}, u32[]{:S(2)}) async-start(bf16[64,144,128]{2,1,0:T(8,128)(2,1)} %pack.1), calls=%async_computation | async-start | bytes 4718592 | tf_op jit(solution)/shard_map/all_to_all | solution.py:404
  103.7 29.0 %copy-start.7 = (bf16[2,24,3072]{2,1,0:T(8,128)(2,1)S(1)}, bf16[2,24,3072]{2,1,0:T(8,128)(2,1)}, u32[]{:S(2)}) copy-start(bf16[2,24,3072]{2,1,0:T(8,128)(2,1)} %get-tuple-element.71) | copy-start | bytes 884740
  108.5 18.9 %collective-permute-start.15 = (bf16[48,3072]{1,0:T(8,128)(2,1)S(1)}, bf16[48,3072]{1,0:T(8,128)(2,1)S(1)}, u32[]{:S(2)}, u32[]{:S(2)}) collective-permute-start(bf16[48,3072]{1,0:T(8,128)(2,1)S(1)} %add_convert_fusion.1), channel_id=1, source_target_pairs={{0,2},{8,10},{2,4},{10,12},{4,6},{12,14},{6,0},{14,8},{1,3},{9,11}... | collective-permute-start | bytes 884744 | tf_op jit(solution)/shard_map/ppermute | solution.py:348
  117.8 14.9 %collective-permute-start.18 = (bf16[48,3072]{1,0:T(8,128)(2,1)S(1)}, bf16[48,3072]{1,0:T(8,128)(2,1)S(1)}, u32[]{:S(2)}, u32[]{:S(2)}) collective-permute-start(bf16[48,3072]{1,0:T(8,128)(2,1)S(1)} %add_convert_fusion), channel_id=1, source_target_pairs={{0,6},{8,14},{2,0},{10,8},{4,2},{12,10},{6,4},{14,12},{1,7},{9,15}... | collective-permute-start | bytes 884744 | tf_op jit(solution)/shard_map/ppermute | solution.py:348
where the time goes:
time: 138 us
  waiting for transfers between devices  43.7 us (32%)
  Pallas kernels  41.4 us (30%)
  starting transfers between devices  34.8 us (25%)
  local copies, waits for them, and re-layouts  9.45 us (7%)
  other arithmetic  7.21 us (5%)
    ppermute x14, waiting for transfers between devices, shift(): lax.ppermute(x, ('zl', 'zh'), [(at(z), at((z + by) % NZ)) for z in range(...  38.1 us
    pallas_call x4, Pallas kernels, kv_call(): pl.pallas_call(functools.partial(kv_kernel, backs, n_att, len(chunks), fi...  36.9 us
    ppermute x14, starting transfers between devices, shift(): lax.ppermute(x, ('zl', 'zh'), [(at(z), at((z + by) % NZ)) for z in range(...  24.1 us
    unnamed x16, local copies, waits for them, and re-layouts  8.3 us
    all_to_all x1, starting transfers between devices, on_device(): lax.all_to_all(outbound, 'xy', split_axis=0, concat_axis=0, tiled=True)  7.04 us
    ppermute x9, waiting for transfers between devices, swap(): return lax.ppermute(x, axis, [(0, 1), (1, 0)])  4.39 us
    ppermute x9, starting transfers between devices, swap(): return lax.ppermute(x, axis, [(0, 1), (1, 0)])  3.65 us
    pallas_call x1, Pallas kernels, pack_call(): pl.pallas_call(functools.partial(pack_kernel, order), out_shape=jax.Shape...  3.13 us
  transfers between devices with their start and end apart: 24, of which 10 were waited for; matrix products, arithmetic and copies ran while one was open for 6% of the time, Pallas kernels for 29%

commit v1 on v0

--- a/solution.py
+++ b/solution.py
@@ -18,6 +18,7 @@
 ROWS = REQ_DEV * SLOT
 HALF = ROWS // 2
 LANES = 128
+MERGE_FLOPS = 3 * 10**10
 VMEM = pl.BlockSpec(memory_space=pltpu.VMEM)
 SMEM = pl.BlockSpec(memory_space=pltpu.SMEM)
 HBM = pl.BlockSpec(memory_space=pltpu.HBM)
@@ -126,14 +127,24 @@
         load(part_scr.at[pl.ds(i * HALF, HALF)], out, sems.at[i])
 
 
-def load_weights(shard, sources, held, sems):
-    wk, wv, wq, wo = sources
-    wkv_v, wq_v, wo_v = held
-    per_dev = wk.shape[1]
-    load(wk, wkv_v.at[shard, :, pl.ds(0, per_dev)], sems.at[shard, 0])
-    load(wv, wkv_v.at[shard, :, pl.ds(per_dev, per_dev)], sems.at[shard, 1])
-    load(wq, wq_v.at[shard], sems.at[shard, 2])
-    load(wo, wo_v.at[pl.ds(shard * per_dev, per_dev)], sems.at[shard, 3])
+def load_keys(weights, wkv_v, sems):
+    per_dev = weights[0].shape[1]
+    for i, w in enumerate(weights):
+        load(w, wkv_v.at[i // 2, :, pl.ds(i % 2 * per_dev, per_dev)], sems.at[i])
+
+
+def load_rest(weights, wq_v, wo_v, sems):
+    wq, wq_p, wo, wo_p = weights
+    per_dev = wq.shape[1]
+    load(wq, wq_v.at[0], sems.at[0])
+    load(wq_p, wq_v.at[1], sems.at[1])
+    load(wo, wo_v.at[pl.ds(0, per_dev)], sems.at[2])
+    load(wo_p, wo_v.at[pl.ds(per_dev, per_dev)], sems.at[3])
+
+
+def rest_landed(wo_v, per_dev, sems):
+    landed(wo_v.at[pl.ds(0, per_dev)], sems.at[2])
+    landed(wo_v.at[pl.ds(per_dev, per_dev)], sems.at[3])
 
 
 def held_shapes(width, per_dev):
@@ -144,24 +155,35 @@
     ]
 
 
-def pinned(held):
-    return [pltpu.with_memory_space_constraint(w, pltpu.VMEM) for w in held]
-
-
-def kv_kernel(backs, n_att, pieces, fill, *refs):
+def pinned(held, space=pltpu.VMEM):
+    return [pltpu.with_memory_space_constraint(w, space) for w in held]
+
+
+def kv_kernel(backs, att, keep, pieces, fill, *refs):
     refs = list(refs)
     take = lambda count: [refs.pop(0) for _ in range(count)]
+    fill_keys, fill_rest = fill
+    n_att = len(att)
+    extra = n_att - len(backs) if n_att else 0
     meta, lens, gain, cosine, sine = take(5)
-    weights = take(8 if fill else 3)
+    key_w = take(4 if fill_keys else 1)
+    rest_w = take((4 if fill_rest else 2) if n_att else 0)
     chunks = take(pieces)
-    wkv_v, wq_v, wo_v = take(3) if fill else weights
+    given = take(3 if extra else 0)
+    (wkv_v,) = take(1) if fill_keys else key_w
+    if n_att:
+        wq_v, wo_v = take(2) if fill_rest else rest_w
     parts = take(2 * n_att)
+    kept = take(3 if keep else 0)
     wires = take(2)
-    g_scr, cos_scr, sin_scr, x_scr, w_scr, wire_scr, small, piece_sem, w_sem, out_sem = take(10)
+    g_scr, cos_scr, sin_scr, x_scr, w_scr, wire_scr, small, piece_sem, key_sem, rest_sem, out_sem, given_sem = take(
+        12
+    )
+    if n_att or keep:
+        k_scr, v_scr = take(2)
     if n_att:
-        k_scr, v_scr = take(2)
         attn_scr, part_scr, part_sem = take(3)
-    per_dev = wq_v.shape[2]
+    per_dev = wkv_v.shape[2] // 2
     tiles = per_dev // LANES
     rows = len(backs) * ROWS
     load(gain, g_scr, small.at[0])
@@ -172,9 +194,16 @@
         at += ref.shape[0]
     load(cosine, cos_scr, small.at[1])
     load(sine, sin_scr, small.at[2])
-    if fill:
-        load_weights(0, weights[:4], (wkv_v, wq_v, wo_v), w_sem)
-        load_weights(1, weights[4:], (wkv_v, wq_v, wo_v), w_sem)
+    handed = []
+    if extra:
+        late = pl.ds(rows, ROWS)
+        handed = [x_scr.at[late], k_scr.at[late], v_scr.at[late]]
+        for i, (src, dst) in enumerate(zip(given, handed)):
+            load(src, dst, given_sem.at[i])
+    if fill_keys:
+        load_keys(key_w, wkv_v, key_sem)
+    if fill_rest:
+        load_rest(rest_w, wq_v, wo_v, rest_sem)
     token = lax.broadcasted_iota(jnp.int32, (SLOT, 1), 0)
     alive = []
     for back in backs:
@@ -182,7 +211,7 @@
         for j in range(REQ_DEV):
             alive.append((token < lens[base + j]).astype(jnp.float32))
     alive = jnp.concatenate(alive, 0)
-    masks = score_masks(backs[:n_att], meta, lens, per_dev // HD) if n_att else []
+    masks = score_masks(att, meta, lens, per_dev // HD) if n_att else []
     landed(g_scr, small.at[0])
     for i, span in enumerate(spans):
         landed(x_scr.at[span], piece_sem.at[i])
@@ -191,18 +220,23 @@
         x_scr[span, :] = (xf * lax.rsqrt(mean_sq + EPS) * g_scr[...]).astype(jnp.bfloat16)
     landed(cos_scr, small.at[1])
     landed(sin_scr, small.at[2])
+    for i, y in enumerate(handed):
+        landed(y, given_sem.at[i])
+    if keep:
+        load(x_scr.at[pl.ds(0, keep * ROWS)], kept[0], small.at[0])
 
     def body(shard, carry):
         cols = columns(shard, per_dev)
-        if fill:
-            landed(wkv_v.at[shard, :, pl.ds(0, per_dev)], w_sem.at[shard, 0])
-            landed(wkv_v.at[shard, :, pl.ds(per_dev, per_dev)], w_sem.at[shard, 1])
-        y = jnp.dot(x_scr[...], wkv_v[shard], preferred_element_type=jnp.float32)
+        if fill_keys:
+            for i in range(2):
+                landed(wkv_v.at[shard, :, pl.ds(i * per_dev, per_dev)], key_sem.at[2 * shard + i])
+        y = jnp.dot(x_scr[:rows, :], wkv_v[shard], preferred_element_type=jnp.float32)
         k = rotate(y[:, :per_dev], cos_scr[...], sin_scr[...]).astype(jnp.bfloat16)
         v = y[:, per_dev:].astype(jnp.bfloat16)
-        if n_att:
-            k_scr[:, cols] = k[: k_scr.shape[0]]
-            v_scr[:, cols] = v[: v_scr.shape[0]]
+        if n_att or keep:
+            count = rows if n_att else keep * ROWS
+            k_scr[:count, cols] = k[:count]
+            v_scr[:count, cols] = v[:count]
         for kv, y in enumerate((k, v)):
             y = jnp.where(alive > 0.5, y.astype(jnp.float32), 0.0)
             for t in range(tiles):
@@ -214,58 +248,79 @@
             def _():
                 load(wire_scr.at[i], wire, out_sem.at[i])
 
-        if fill:
-            landed(wq_v.at[shard], w_sem.at[shard, 2])
+        if fill_rest:
+            landed(wq_v.at[shard], rest_sem.at[shard])
         if n_att:
             attend_shard(shard, masks, x_scr, k_scr, v_scr, wq_v, cos_scr[...], sin_scr[...], attn_scr)
         return carry
 
     lax.fori_loop(0, 2, body, 0)
-    if fill:
-        landed(wo_v.at[pl.ds(0, per_dev)], w_sem.at[0, 3])
-        landed(wo_v.at[pl.ds(per_dev, per_dev)], w_sem.at[1, 3])
+    if keep:
+        load(k_scr, kept[1], small.at[1])
+        load(v_scr, kept[2], small.at[2])
+    if fill_rest:
+        rest_landed(wo_v, per_dev, rest_sem)
     if n_att:
         project(attn_scr, wo_v, part_scr, parts, part_sem)
         for i, part in enumerate(parts):
             landed(part, part_sem.at[i])
     for i, wire in enumerate(wires):
         landed(wire, out_sem.at[i])
-
-
-def kv_call(backs, n_att, meta, lens, tables, weights, chunks):
+    for i, y in enumerate(kept):
+        landed(y, small.at[i])
+
+
+def kv_call(backs, att, keep, meta, lens, tables, key_w, rest_w, chunks, given):
     n = len(backs)
-    fill = len(weights) == 8
-    width, per_dev = weights[0].shape if fill else weights[1].shape[1:]
+    n_att = len(att)
+    fill = (len(key_w) == 4, n_att > 0 and len(rest_w) == 4)
+    width, per_dev = key_w[0].shape if fill[0] else (key_w[0].shape[1], key_w[0].shape[2] // 2)
     per_req = SLOT * 2 * per_dev // LANES
     bf16 = lambda *shape: jax.ShapeDtypeStruct(shape, jnp.bfloat16)
     scr = lambda *shape: pltpu.VMEM(shape, jnp.bfloat16)
-    outs = (held_shapes(width, per_dev) if fill else []) + [bf16(HALF, width)] * (2 * n_att)
+    held = held_shapes(width, per_dev)
+    outs = held[:1] * fill[0] + held[1:] * fill[1]
+    n_held = len(outs)
+    outs += [bf16(HALF, width)] * (2 * n_att)
+    if keep:
+        outs += [bf16(keep * ROWS, width)] + [bf16(keep * ROWS, 2 * per_dev)] * 2
     outs += [bf16(n * REQ_DEV * per_req, LANES)] * 2
     dma = pltpu.SemaphoreType.DMA
     scratch = [pltpu.VMEM(y.shape, y.dtype) for y in tables]
     scratch += [
-        scr(n * ROWS, width),
+        scr(max(n, n_att) * ROWS, width),
         pltpu.VMEM((n * REQ_DEV * per_req, LANES), jnp.float32),
         scr(2, n * REQ_DEV * per_req, LANES),
         dma((3,)),
         dma((len(chunks),)),
-        dma((2, 4)),
+        dma((4,)),
+        dma((4,)),
         dma((2,)),
+        dma((3,)),
     ]
+    local = max(n_att, keep)
+    if local:
+        scratch += [scr(local * ROWS, 2 * per_dev)] * 2
     if n_att:
-        scratch += [scr(n_att * ROWS, 2 * per_dev)] * 3 + [scr(n_att * ROWS, width), dma((2 * n_att,))]
+        scratch += [scr(n_att * ROWS, 2 * per_dev), scr(n_att * ROWS, width), dma((2 * n_att,))]
+    key_w = key_w if fill[0] else pinned(key_w)
+    rest_w = rest_w if fill[1] else pinned(rest_w) if n_att else []
     res = pl.pallas_call(
-        functools.partial(kv_kernel, backs, n_att, len(chunks), fill),
+        functools.partial(kv_kernel, backs, att, keep, len(chunks), fill),
         out_shape=outs,
-        in_specs=[SMEM, SMEM] + [HBM] * 3 + ([HBM] * 8 if fill else [VMEM] * 3) + [HBM] * len(chunks),
-        out_specs=[VMEM] * (3 * fill) + [HBM] * (len(outs) - 3 * fill),
+        in_specs=[SMEM, SMEM]
+        + [HBM] * 3
+        + [HBM if fill[0] else VMEM] * len(key_w)
+        + [HBM if fill[1] else VMEM] * len(rest_w)
+        + [HBM] * (len(chunks) + len(given)),
+        out_specs=[VMEM] * n_held + [HBM] * (len(outs) - n_held),
         scratch_shapes=scratch,
         compiler_params=pltpu.CompilerParams(vmem_limit_bytes=24 << 20),
         cost_estimate=pl.CostEstimate(
             flops=(n + n_att) * ROWS * width * per_dev // 4, bytes_accessed=1 << 18, transcendentals=0
         ),
         name="keys",
-    )(meta, lens, *tables, *(weights if fill else pinned(weights)), *chunks)
+    )(meta, lens, *pinned(tables, pltpu.HBM), *key_w, *rest_w, *chunks, *given)
     wire = [r.reshape(n * REQ_DEV, per_req, LANES) for r in res[-2:]]
     return res[:-2], wire[0], wire[1]
 
@@ -301,7 +356,7 @@
     rows = empty.shape[0]
     return pl.pallas_call(
         functools.partial(pack_kernel, order),
-        out_shape=jax.ShapeDtypeStruct((rows, per_req, LANES), jnp.bfloat16),
+        out_shape=pltpu.HBM((rows, per_req, LANES), jnp.bfloat16),
         in_specs=[SMEM] * 3 + [HBM] * len(wires),
         out_specs=HBM,
         scratch_shapes=[pltpu.VMEM(w.shape, w.dtype) for w in wires]
@@ -337,6 +392,43 @@
         compiler_params=pltpu.CompilerParams(vmem_limit_bytes=8 << 20),
         name="place",
     )(wire)
+
+
+def merge_kernel(a, b, c, d, out_t, out_b):
+    out_t[...] = (a[...].astype(jnp.float32) + b[...].astype(jnp.float32)).astype(out_t.dtype)
+    out_b[...] = (c[...].astype(jnp.float32) + d[...].astype(jnp.float32)).astype(out_b.dtype)
+
+
+def merge_call(top, passing_t, bottom, passing_b):
+    return pl.pallas_call(
+        merge_kernel,
+        out_shape=[jax.ShapeDtypeStruct(top.shape, top.dtype)] * 2,
+        in_specs=[VMEM] * 4,
+        out_specs=[VMEM] * 2,
+        cost_estimate=pl.CostEstimate(flops=MERGE_FLOPS, bytes_accessed=1 << 18, transcendentals=0),
+        name="merge",
+    )(top, passing_t, bottom, passing_b)
+
+
+def finish_kernel(x, *refs):
+    *terms, out = refs
+    for half in range(2):
+        rows = slice(half * HALF, (half + 1) * HALF)
+        total = x[rows, :].astype(jnp.float32)
+        for term in terms[half::2]:
+            total = total + term[...].astype(jnp.float32)
+        out[rows, :] = total.astype(out.dtype)
+
+
+def finish_call(flat, terms):
+    return pl.pallas_call(
+        finish_kernel,
+        out_shape=jax.ShapeDtypeStruct(flat.shape, flat.dtype),
+        in_specs=[VMEM] * (1 + len(terms)),
+        out_specs=VMEM,
+        cost_estimate=pl.CostEstimate(flops=flat.size, bytes_accessed=1 << 18, transcendentals=0),
+        name="finish",
+    )(flat, *terms)
 
 
 def swap(x, axis):
@@ -371,8 +463,8 @@
     tables = (norm_gain.reshape(1, width), *rope_tables(per_dev))
     order, wires = [], []
 
-    def keys(backs, n_att, weights, chunks):
-        extra, own, other = kv_call(backs, n_att, meta, lens, tables, weights, chunks)
+    def keys(backs, att, keep, key_w, rest_w, chunks, given=()):
+        extra, own, other = kv_call(backs, att, keep, meta, lens, tables, key_w, rest_w, chunks, given)
         order.append((backs, 0))
         wires.append(own)
         order.append((backs, 1))
@@ -381,33 +473,31 @@
 
     u1, d1 = shift(flat, 1), shift(flat, -1)
     wk_p, wv_p = swap(w_k, "core"), swap(w_v, "core")
-    wk_p, wq_late, wo_late = bar((wk_p, w_q, w_o))
-    u1, d1, meta, lens, slots, empty = bar((u1, d1, meta, lens, slots, empty))
+    u1, d1, meta, lens, slots, empty, wq_late, wo_late = bar((u1, d1, meta, lens, slots, empty, w_q, w_o))
     u2, d2 = shift(u1, 1), shift(d1, -1)
-    wq_p, wo_p = swap(wq_late, "core"), swap(wo_late, "core")
-    weights = (w_k, w_v, w_q, w_o, wk_p, wv_p, wq_p, wo_p)
-    extra, done = keys((0, 1, -1), 1, weights, (flat, u1, d1))
-    held, part0 = extra[:3], extra[3:]
+    rest = (*pinned((w_q,), pltpu.HBM), swap(wq_late, "core"), *pinned((w_o,), pltpu.HBM), swap(wo_late, "core"))
+    first = (*pinned((w_k, w_v), pltpu.HBM), wk_p, wv_p)
+    (held, *kept), done = keys((0, 1, -1), (), 1, first, (), (*pinned((flat,), pltpu.HBM), u1, d1))
     u2, d2, done = bar((u2, d2, done))
     wires[0] = done
     u3, d3 = shift(u2, 1), shift(d2, -1)
-    (top1, bottom1, top2, bottom2), done = keys((2, -2), 2, held, (u2, d2))
+    extra, done = keys((2, -2), (2, -2, 0), 0, (held,), rest, (u2, d2), kept)
+    held_rest, (top1, bottom1, top2, bottom2, *part0) = extra[:2], extra[2:]
     u3, d3, done = bar((u3, d3, done))
     wires[2] = done
     far = shift(u3[:HALF], 1), shift(d3[HALF:], -1)
-    _, done = keys((3, -3), 0, held, (u3, d3))
+    _, done = keys((3, -3), (), 0, (held,), (), (u3, d3))
     wires[4] = done
-    near_t, near_b = shift(top1, -2), shift(bottom2, 2)
-    (top3, bottom3), _ = keys((4,), 1, held, far)
+    (top3, bottom3), _ = keys((4,), (4,), 0, (held,), held_rest, far)
     passing_t, passing_b = shift(top3, 2), shift(bottom3, -2)
     outbound = pack_call(order, meta, slots, empty, wires)
     inbound = lax.all_to_all(outbound, "xy", split_axis=0, concat_axis=0, tiled=True)
-    add = lambda *ys: sum(y.astype(jnp.float32) for y in ys)
-    merged_t = shift(add(top2, passing_t).astype(jnp.bfloat16), 2)
-    merged_b = shift(add(bottom1, passing_b).astype(jnp.bfloat16), -2)
-    top = add(flat[:HALF], part0[0], near_t, merged_t)
-    bottom = add(flat[HALF:], part0[1], near_b, merged_b)
-    hidden_out = jnp.concatenate([top, bottom]).astype(jnp.bfloat16).reshape(hidden_in.shape)
+    top1, bottom2, outbound = bar((top1, bottom2, outbound))
+    near_t, near_b = shift(top1, -2), shift(bottom2, 2)
+    top2, bottom1 = merge_call(top2, passing_t, bottom1, passing_b)
+    merged_t, merged_b = shift(top2, 2), shift(bottom1, -2)
+    terms = (*part0, near_t, near_b, merged_t, merged_b)
+    hidden_out = finish_call(flat, terms).reshape(hidden_in.shape)
     return hidden_out, place_call(inbound, per_dev)
 
 

time: 138 us -> 125 us (0.906)
  the two profiles are of different devices: /device:TPU:32 before, /device:TPU:1 now
where the time goes in v1:
time: 125 us; the launch traced here: 124 us
  Pallas kernels  45.1 us (36%)
  starting transfers between devices  37.5 us (30%)
  waiting for transfers between devices  36.3 us (29%)
  other arithmetic  3.64 us (3%)
    pallas_call x4, Pallas kernels, kv_call(): pl.pallas_call(functools.partial(kv_kernel, backs, att, keep, len(chunks)...  35.8 us
    ppermute x14, starting transfers between devices, shift(): lax.ppermute(x, ('zl', 'zh'), [(at(z), at((z + by) % NZ)) for z in range(...  24.9 us
    ppermute x14, waiting for transfers between devices, shift(): lax.ppermute(x, ('zl', 'zh'), [(at(z), at((z + by) % NZ)) for z in range(...  21 us
    ppermute x9, waiting for transfers between devices, swap(): return lax.ppermute(x, axis, [(0, 1), (1, 0)])  7.9 us
    all_to_all x1, waiting for transfers between devices, on_device(): lax.all_to_all(outbound, 'xy', split_axis=0, concat_axis=0, tiled=True)  7.39 us
    all_to_all x1, starting transfers between devices, on_device(): lax.all_to_all(outbound, 'xy', split_axis=0, concat_axis=0, tiled=True)  6.79 us
    ppermute x9, starting transfers between devices, swap(): return lax.ppermute(x, axis, [(0, 1), (1, 0)])  5.78 us
    pallas_call x1, Pallas kernels, pack_call(): pl.pallas_call(functools.partial(pack_kernel, order), out_shape=pltpu.HBM...  3.13 us
  transfers between devices with their start and end apart: 24, of which 11 were waited for; matrix products, arithmetic and copies ran while one was open for 3% of the time, Pallas kernels for 35%

profile of v1, /device:TPU:1, one launch (start us, length us, event | category | flops | bytes accessed | tf_op | source)
XLA Modules:
  0.0 123.9 jit_solution(12206464081383337441)
XLA Ops:
  0.6 2.5 %collective-permute-start = (bf16[96,3072]{1,0:T(8,128)(2,1)}, bf16[96,3072]{1,0:T(8,128)(2,1)S(1)}, u32[]{:S(2)}, u32[]{:S(2)}) collective-permute-start(bf16[96,3072]{1,0:T(8,128)(2,1)} %bitcast.28), channel_id=1, source_target_pairs={{0,8},{8,2},{2,10},{10,4},{4,12},{12,6},{6,14},{14,0},{1,9},{9,3},... | collective-permute-start | bytes 1769480 | tf_op jit(solution)/shard_map/ppermute | solution.py:440
  3.2 4.0 %collective-permute-start.1 = (bf16[96,3072]{1,0:T(8,128)(2,1)}, bf16[96,3072]{1,0:T(8,128)(2,1)S(1)}, u32[]{:S(2)}, u32[]{:S(2)}) collective-permute-start(bf16[96,3072]{1,0:T(8,128)(2,1)} %bitcast.29), channel_id=1, source_target_pairs={{0,14},{8,0},{2,8},{10,2},{4,10},{12,4},{6,12},{14,6},{1,15},{9,1}... | collective-permute-start | bytes 1769480 | tf_op jit(solution)/shard_map/ppermute | solution.py:440
  7.2 1.3 %pad_add_fusion.1 = s32[64]{0:T(128)} fusion(s32[32]{0:T(128)} %bitcast.38, s32[32]{0:T(128)} %bitcast.40), kind=kLoop, calls=%fused_computation.12 | loop fusion | flops 64 | bytes 512 | tf_op jit(solution)/shard_map/concatenate | solution.py:448
  8.5 1.0 collective-permute-start.3
  9.5 0.7 fusion.1
  10.2 0.5 iota_multiply_fusion
  10.7 0.1 pad_add_fusion.refs_0_.meta
  10.8 6.9 %collective-permute-done.2 = s32[64]{0:T(128)S(1)} collective-permute-done((s32[64]{0:T(128)}, s32[64]{0:T(128)S(1)}, u32[]{:S(2)}, u32[]{:S(2)}) %collective-permute-start.2) | collective-permute-done | bytes 288 | tf_op jit(solution)/shard_map/ppermute | solution.py:435
  17.8 0.2 convert_reduce_fusion
  18.0 0.7 compare_select_fusion
  18.7 0.1 reshape.68.slots
  18.7 0.1 reshape.67.refs_1_
  18.8 0.1 fusion
  18.9 1.4 %collective-permute-done.refs_10_ = bf16[96,3072]{1,0:T(8,128)(2,1)S(1)} collective-permute-done((bf16[96,3072]{1,0:T(8,128)(2,1)}, bf16[96,3072]{1,0:T(8,128)(2,1)S(1)}, u32[]{:S(2)}, u32[]{:S(2)}) %collective-permute-start) | collective-permute-done | bytes 589856 | tf_op jit(solution)/shard_map/ppermute | solution.py:440
  20.4 1.2 collective-permute-start.5
  21.6 3.0 %collective-permute-start.8 = (bf16[96,3072]{1,0:T(8,128)(2,1)S(1)}, bf16[96,3072]{1,0:T(8,128)(2,1)S(1)}, u32[]{:S(2)}, u32[]{:S(2)}) collective-permute-start(bf16[96,3072]{1,0:T(8,128)(2,1)S(1)} %collective-permute-done.1.refs_11_), channel_id=1, source_target_pairs={{0,14},{8,0},{2,8},{10,2},{4,10},{12,4},{6,12},{14,6},{1,15},{9,1}... | collective-permute-start | bytes 1769480 | tf_op jit(solution)/shard_map/ppermute | solution.py:440
  24.6 7.9 %keys.4 = (bf16[2,3072,768]{2,1,0:T(8,128)(2,1)S(1)}, bf16[96,3072]{1,0:T(8,128)(2,1)S(1)}, bf16[96,768]{1,0:T(8,128)(2,1)S(1)}, bf16[96,768]{1,0:T(8,128)(2,1)S...) custom-call(s32[2]{0:T(128)S(1)} %pad_add_fusion.refs_0_.meta, s32[64]{0:T(128)S(1)} %reshape.67.refs_1_, ...), custom_call_target="tpu_custom_call" | custom-call | flops 84934656 | bytes 262144 | tf_op jit(solution)/shard_map/keys/pallas_call | solution.py:308
  32.5 5.3 %collective-permute-done.7.refs_10_ = bf16[96,3072]{1,0:T(8,128)(2,1)S(1)} collective-permute-done((bf16[96,3072]{1,0:T(8,128)(2,1)S(1)}, bf16[96,3072]{1,0:T(8,128)(2,1)S(1)}, u32[]{:S(2)}, u32[]{:S(2)}) %collective-permute-start.7) | collective-permute-done | bytes 589856 | tf_op jit(solution)/shard_map/ppermute | solution.py:440
  37.8 0.5 collective-permute-done.8.refs_11_
  38.4 1.1 collective-permute-start.10
  39.5 1.5 %collective-permute-start.11 = (bf16[96,3072]{1,0:T(8,128)(2,1)S(1)}, bf16[96,3072]{1,0:T(8,128)(2,1)S(1)}, u32[]{:S(2)}, u32[]{:S(2)}) collective-permute-start(bf16[96,3072]{1,0:T(8,128)(2,1)S(1)} %collective-permute-done.8.refs_11_), channel_id=1, source_target_pairs={{0,14},{8,0},{2,8},{10,2},{4,10},{12,4},{6,12},{14,6},{1,15},{9,1}... | collective-permute-start | bytes 1769480 | tf_op jit(solution)/shard_map/ppermute | solution.py:440
  41.1 14.0 %keys.5 = (bf16[2,3072,384]{2,1,0:T(8,128)(2,1)S(1)}, bf16[768,3072]{1,0:T(8,128)(2,1)S(1)}, bf16[48,3072]{1,0:T(8,128)(2,1)S(1)}, bf16[48,3072]{1,0:T(8,128)(2,...) custom-call(s32[2]{0:T(128)S(1)} %pad_add_fusion.refs_0_.meta, ...), custom_call_target="tpu_custom_call" | custom-call | flops 141557760 | bytes 262144 | tf_op jit(solution)/shard_map/keys/pallas_call | solution.py:308
  55.1 0.1 collective-permute-start.14
  55.3 2.7 %collective-permute-start.15 = (bf16[48,3072]{1,0:T(8,128)(2,1)S(1)}, bf16[48,3072]{1,0:T(8,128)(2,1)S(1)}, u32[]{:S(2)}, u32[]{:S(2)}) collective-permute-start(bf16[48,3072]{1,0:T(8,128)(2,1)S(1)} %slice.15), channel_id=1, source_target_pairs={{0,14},{8,0},{2,8},{10,2},{4,10},{12,4},{6,12},{14,6},{1,15},{9,1}... | collective-permute-start | bytes 884744 | tf_op jit(solution)/shard_map/ppermute | solution.py:440
  58.0 2.4 %collective-permute-start.9 = (bf16[12,144,128]{2,1,0:T(8,128)(2,1)S(1)}, bf16[12,144,128]{2,1,0:T(8,128)(2,1)S(1)}, u32[]{:S(2)}, u32[]{:S(2)}) collective-permute-start(bf16[12,144,128]{2,1,0:T(8,128)(2,1)S(1)} %bitcast.24), channel_id=1, source_target_pairs={{0,1},{1,0},{2,3},{3,2},{4,5},{5,4},{6,7},{7,6},{8,9},{9,8},{10,11... | collective-permute-start | bytes 1327112 | tf_op jit(solution)/shard_map/ppermute | solution.py:435
  60.4 4.8 %keys.6 = (bf16[1152,128]{1,0:T(8,128)(2,1)S(1)}, bf16[1152,128]{1,0:T(8,128)(2,1)S(1)}) custom-call(s32[2]{0:T(128)S(1)} %pad_add_fusion.refs_0_.meta, s32[64]{0:T(128)S(1)} %reshape.67.refs_1_, f32[1,3072]{1,0:T(1,128)} %bitcast.35, f32[24,384]{1,0:T(8,128)} %constant.49.clone.refs_3_, f32[24,384]{1,0:T(8,128)} %constant.50.clone.refs_4_, ...), custom_call_target="tpu_custom_call" | custom-call | flops 56623104 | bytes 262144 | tf_op jit(solution)/shard_map/keys/pallas_call | solution.py:308
  65.2 0.1 collective-permute-start.13
  65.3 0.5 collective-permute-start.12
  65.8 9.1 %keys.7 = (bf16[48,3072]{1,0:T(8,128)(2,1)}, bf16[48,3072]{1,0:T(8,128)(2,1)S(1)}, bf16[576,128]{1,0:T(8,128)(2,1)S(1)}, bf16[576,128]{1,0:T(8,128)(2,1)S(1)}) custom-call(s32[2]{0:T(128)S(1)} %pad_add_fusion.refs_0_.meta, s32[64]{0:T(128)S(1)} %reshape.67.refs_1_, f32[1,3072]{1,0:T(1,128)} %bitcast.36, f32[24,384]{1,0:T(8,128)} %constant.49.clone.refs_3_, ...), custom_call_target="tpu_custom_call" | custom-call | flops 56623104 | bytes 262144 | tf_op jit(solution)/shard_map/keys/pallas_call | solution.py:308
  74.9 0.8 collective-permute-start.19
  75.8 3.1 %collective-permute-start.20 = (bf16[48,3072]{1,0:T(8,128)(2,1)S(1)}, bf16[48,3072]{1,0:T(8,128)(2,1)}, u32[]{:S(2)}, u32[]{:S(2)}) collective-permute-start(bf16[48,3072]{1,0:T(8,128)(2,1)S(1)} %get-tuple-element.79), channel_id=1, source_target_pairs={{0,6},{8,14},{2,0},{10,8},{4,2},{12,10},{6,4},{14,12},{1,7},{9,15}... | collective-permute-start | bytes 884744 | tf_op jit(solution)/shard_map/ppermute | solution.py:440
  78.8 0.6 collective-permute-start.16
  79.5 1.0 collective-permute-done.16.refs_7_
  80.5 3.1 %pack.1 = bf16[64,144,128]{2,1,0:T(8,128)(2,1)} custom-call(s32[2]{0:T(128)S(1)} %pad_add_fusion.refs_0_.meta, s32[64]{0:T(128)S(1)} %reshape.68.slots, s32[64]{0:T(128)S(1)} %convert_subtract_fusion.empty, bf16[12,144,128]{2,1,0:T(8,128)(2,1)S(1)} %bitcast.20, bf16[12,144,128]{2,1,0:T(8,128)(2,1)S(1)} %collective-permute-done.9.refs_1_, ...), custom_call_target="tpu_custom_call" | custom-call | bytes 262144 | tf_op jit(solution)/shard_map/pack/pallas_call | solution.py:357
  83.6 6.8 %all-to-all-start = ((bf16[64,144,128]{2,1,0:T(8,128)(2,1)}), bf16[64,144,128]{2,1,0:T(8,128)(2,1)S(1)}, u32[]{:S(2)}, u32[]{:S(2)}) async-start(bf16[64,144,128]{2,1,0:T(8,128)(2,1)} %pack.1), calls=%async_computation | async-start | bytes 4718592 | tf_op jit(solution)/shard_map/all_to_all | solution.py:494
  90.4 0.6 collective-permute-start.17
  91.0 1.8 %collective-permute-start.18 = (bf16[48,3072]{1,0:T(8,128)(2,1)S(1)}, bf16[48,3072]{1,0:T(8,128)(2,1)}, u32[]{:S(2)}, u32[]{:S(2)}) collective-permute-start(bf16[48,3072]{1,0:T(8,128)(2,1)S(1)} %get-tuple-element.75), channel_id=1, source_target_pairs={{0,2},{8,10},{2,4},{10,12},{4,6},{12,14},{6,0},{14,8},{1,3},{9,11}... | collective-permute-start | bytes 884744 | tf_op jit(solution)/shard_map/ppermute | solution.py:440
  92.8 0.5 collective-permute-done.20.d
  93.4 2.1 %merge.1 = (bf16[48,3072]{1,0:T(8,128)(2,1)}, bf16[48,3072]{1,0:T(8,128)(2,1)}) custom-call(bf16[48,3072]{1,0:T(8,128)(2,1)} %copy-done.3, bf16[48,3072]{1,0:T(8,128)(2,1)} %collective-permute-done.19.b, bf16[48,3072]{1,0:T(8,128)(2,1)} %copy-done.2, bf16[48,3072]{1,0:T(8,128)(2,1)} %collective-permute-done.20.d), custom_call_target="tpu_custom_call" | custom-call | flops 30000001024 | bytes 262144 | tf_op jit(solution)/shard_map/merge/pallas_call | solution.py:403
  95.5 1.5 %collective-permute-start.21 = (bf16[48,3072]{1,0:T(8,128)(2,1)}, bf16[48,3072]{1,0:T(8,128)(2,1)S(1)}, u32[]{:S(2)}, u32[]{:S(2)}) collective-permute-start(bf16[48,3072]{1,0:T(8,128)(2,1)} %get-tuple-element.80), channel_id=1, source_target_pairs={{0,2},{8,10},{2,4},{10,12},{4,6},{12,14},{6,0},{14,8},{1,3},{9,11}... | collective-permute-start | bytes 884744 | tf_op jit(solution)/shard_map/ppermute | solution.py:440
  97.0 2.1 %collective-permute-start.22 = (bf16[48,3072]{1,0:T(8,128)(2,1)}, bf16[48,3072]{1,0:T(8,128)(2,1)}, u32[]{:S(2)}, u32[]{:S(2)}) collective-permute-start(bf16[48,3072]{1,0:T(8,128)(2,1)} %get-tuple-element.81), channel_id=1, source_target_pairs={{0,6},{8,14},{2,0},{10,8},{4,2},{12,10},{6,4},{14,12},{1,7},{9,15}... | collective-permute-start | bytes 884744 | tf_op jit(solution)/shard_map/ppermute | solution.py:440
  99.1 2.8 %collective-permute-done.17.refs_2_ = bf16[48,3072]{1,0:T(8,128)(2,1)S(1)} collective-permute-done((bf16[48,3072]{1,0:T(8,128)(2,1)S(1)}, bf16[48,3072]{1,0:T(8,128)(2,1)S(1)}, u32[]{:S(2)}, u32[]{:S(2)}) %collective-permute-start.17) | collective-permute-done | bytes 294944 | tf_op jit(solution)/shard_map/ppermute | solution.py:440
  101.9 0.3 collective-permute-done.18.refs_3_
  102.2 8.2 %collective-permute-done.21.refs_4_ = bf16[48,3072]{1,0:T(8,128)(2,1)S(1)} collective-permute-done((bf16[48,3072]{1,0:T(8,128)(2,1)}, bf16[48,3072]{1,0:T(8,128)(2,1)S(1)}, u32[]{:S(2)}, u32[]{:S(2)}) %collective-permute-start.21) | collective-permute-done | bytes 294944 | tf_op jit(solution)/shard_map/ppermute | solution.py:440
  110.4 1.8 %collective-permute-done.22.refs_5_ = bf16[48,3072]{1,0:T(8,128)(2,1)} collective-permute-done((bf16[48,3072]{1,0:T(8,128)(2,1)}, bf16[48,3072]{1,0:T(8,128)(2,1)}, u32[]{:S(2)}, u32[]{:S(2)}) %collective-permute-start.22) | collective-permute-done | bytes 294944 | tf_op jit(solution)/shard_map/ppermute | solution.py:440
  112.2 2.7 %finish.1 = bf16[96,3072]{1,0:T(8,128)(2,1)} custom-call(bf16[96,3072]{1,0:T(8,128)(2,1)} %bitcast.31, bf16[48,3072]{1,0:T(8,128)(2,1)} %copy-done, bf16[48,3072]{1,0:T(8,128)(2,1)} %copy-done.1, bf16[48,3072]{1,0:T(8,128)(2,1)} %copy-done.4, bf16[48,3072]{1,0:T(8,128)(2,1)} %collective-permute-done.18.refs_3_, bf16[48,3072]{1,0:T(8,128)(2,1)} %copy-done.5, ...), custom_call_target="tpu_custom_call" | custom-call | flops 294912 | bytes 262144 | tf_op jit(solution)/shard_map/finish/pallas_call | solution.py:424
  114.9 7.4 %all-to-all-done = bf16[64,144,128]{2,1,0:T(8,128)(2,1)S(1)} async-done(((bf16[64,144,128]{2,1,0:T(8,128)(2,1)}), bf16[64,144,128]{2,1,0:T(8,128)(2,1)S(1)}, u32[]{:S(2)}, u32[]{:S(2)}) %all-to-all-start) | async-done | bytes 2359328 | tf_op jit(solution)/shard_map/all_to_all | solution.py:494
  122.3 1.4 %place.1 = bf16[64,24,2,384]{3,2,1,0:T(2,128)(2,1)} custom-call(bf16[64,24,3,2,128]{4,3,2,1,0:T(2,128)(2,1)S(1)} %bitcast.19), custom_call_target="tpu_custom_call" | custom-call | tf_op jit(solution)/shard_map/place/pallas_call | solution.py:386
  (35 shorter events, 0.2 us)
Async XLA Ops:
  0.6 19.7 %collective-permute-start = (bf16[96,3072]{1,0:T(8,128)(2,1)}, bf16[96,3072]{1,0:T(8,128)(2,1)S(1)}, u32[]{:S(2)}, u32[]{:S(2)}) collective-permute-start(bf16[96,3072]{1,0:T(8,128)(2,1)} %bitcast.28), channel_id=1, source_target_pairs={{0,8},{8,2},{2,10},{10,4},{4,12},{12,6},{6,14},{14,0},{1,9},{9,3},... | collective-permute-start | bytes 1769480 | tf_op jit(solution)/shard_map/ppermute | solution.py:440
  3.2 17.2 %collective-permute-start.1 = (bf16[96,3072]{1,0:T(8,128)(2,1)}, bf16[96,3072]{1,0:T(8,128)(2,1)S(1)}, u32[]{:S(2)}, u32[]{:S(2)}) collective-permute-start(bf16[96,3072]{1,0:T(8,128)(2,1)} %bitcast.29), channel_id=1, source_target_pairs={{0,14},{8,0},{2,8},{10,2},{4,10},{12,4},{6,12},{14,6},{1,15},{9,1}... | collective-permute-start | bytes 1769480 | tf_op jit(solution)/shard_map/ppermute | solution.py:440
  8.5 9.2 %collective-permute-start.2 = (s32[64]{0:T(128)}, s32[64]{0:T(128)S(1)}, u32[]{:S(2)}, u32[]{:S(2)}) collective-permute-start(s32[64]{0:T(128)} %pad_add_fusion.1), channel_id=1, source_target_pairs={{0,8},{8,0},{1,9},{9,1},{2,10},{10,2},{3,11},{11,3},{4,12},{12,4},... | collective-permute-start | bytes 776 | tf_op jit(solution)/shard_map/ppermute | solution.py:435
  8.5 13.1 %collective-permute-start.3 = (bf16[3072,384]{1,0:T(8,128)(2,1)}, bf16[3072,384]{1,0:T(8,128)(2,1)S(1)}, u32[]{:S(2)}, u32[]{:S(2)}) collective-permute-start(bf16[3072,384]{1,0:T(8,128)(2,1)} %refs_5_.1), channel_id=1, source_target_pairs={{0,1},{1,0},{2,3},{3,2},{4,5},{5,4},{6,7},{7,6},{8,9},{9,8},{10,11... | collective-permute-start | bytes 7077896 | tf_op jit(solution)/shard_map/ppermute | solution.py:435
  9.5 15.1 %collective-permute-start.4 = (bf16[3072,384]{1,0:T(8,128)(2,1)}, bf16[3072,384]{1,0:T(8,128)(2,1)}, u32[]{:S(2)}, u32[]{:S(2)}) collective-permute-start(bf16[3072,384]{1,0:T(8,128)(2,1)} %refs_6_.2), channel_id=1, source_target_pairs={{0,1},{1,0},{2,3},{3,2},{4,5},{5,4},{6,7},{7,6},{8,9},{9,8},{10,11... | collective-permute-start | bytes 7077896 | tf_op jit(solution)/shard_map/ppermute | solution.py:435
  20.4 20.7 %collective-permute-start.5 = (bf16[3072,384]{1,0:T(8,128)(2,1)}, bf16[3072,384]{1,0:T(8,128)(2,1)S(1)}, u32[]{:S(2)}, u32[]{:S(2)}) collective-permute-start(bf16[3072,384]{1,0:T(8,128)(2,1)} %refs_6_.3), channel_id=1, source_target_pairs={{0,1},{1,0},{2,3},{3,2},{4,5},{5,4},{6,7},{7,6},{8,9},{9,8},{10,11... | collective-permute-start | bytes 7077896 | tf_op jit(solution)/shard_map/ppermute | solution.py:435
  21.6 19.5 %collective-permute-start.6 = (bf16[384,3072]{1,0:T(8,128)(2,1)}, bf16[384,3072]{1,0:T(8,128)(2,1)S(1)}, u32[]{:S(2)}, u32[]{:S(2)}) collective-permute-start(bf16[384,3072]{1,0:T(8,128)(2,1)} %refs_8_.1), channel_id=1, source_target_pairs={{0,1},{1,0},{2,3},{3,2},{4,5},{5,4},{6,7},{7,6},{8,9},{9,8},{10,11... | collective-permute-start | bytes 7077896 | tf_op jit(solution)/shard_map/ppermute | solution.py:435
  21.6 16.2 %collective-permute-start.7 = (bf16[96,3072]{1,0:T(8,128)(2,1)S(1)}, bf16[96,3072]{1,0:T(8,128)(2,1)S(1)}, u32[]{:S(2)}, u32[]{:S(2)}) collective-permute-start(bf16[96,3072]{1,0:T(8,128)(2,1)S(1)} %collective-permute-done.refs_10_), channel_id=1, source_target_pairs={{0,8},{8,2},{2,10},{10,4},{4,12},{12,6},{6,14},{14,0},{1,9},{9,3},... | collective-permute-start | bytes 1769480 | tf_op jit(solution)/shard_map/ppermute | solution.py:440
  21.6 16.8 %collective-permute-start.8 = (bf16[96,3072]{1,0:T(8,128)(2,1)S(1)}, bf16[96,3072]{1,0:T(8,128)(2,1)S(1)}, u32[]{:S(2)}, u32[]{:S(2)}) collective-permute-start(bf16[96,3072]{1,0:T(8,128)(2,1)S(1)} %collective-permute-done.1.refs_11_), channel_id=1, source_target_pairs={{0,14},{8,0},{2,8},{10,2},{4,10},{12,4},{6,12},{14,6},{1,15},{9,1}... | collective-permute-start | bytes 1769480 | tf_op jit(solution)/shard_map/ppermute | solution.py:440
  38.4 16.7 %collective-permute-start.10 = (bf16[96,3072]{1,0:T(8,128)(2,1)S(1)}, bf16[96,3072]{1,0:T(8,128)(2,1)S(1)}, u32[]{:S(2)}, u32[]{:S(2)}) collective-permute-start(bf16[96,3072]{1,0:T(8,128)(2,1)S(1)} %collective-permute-done.7.refs_10_), channel_id=1, source_target_pairs={{0,8},{8,2},{2,10},{10,4},{4,12},{12,6},{6,14},{14,0},{1,9},{9,3},... | collective-permute-start | bytes 1769480 | tf_op jit(solution)/shard_map/ppermute | solution.py:440
  39.5 15.6 %collective-permute-start.11 = (bf16[96,3072]{1,0:T(8,128)(2,1)S(1)}, bf16[96,3072]{1,0:T(8,128)(2,1)S(1)}, u32[]{:S(2)}, u32[]{:S(2)}) collective-permute-start(bf16[96,3072]{1,0:T(8,128)(2,1)S(1)} %collective-permute-done.8.refs_11_), channel_id=1, source_target_pairs={{0,14},{8,0},{2,8},{10,2},{4,10},{12,4},{6,12},{14,6},{1,15},{9,1}... | collective-permute-start | bytes 1769480 | tf_op jit(solution)/shard_map/ppermute | solution.py:440
  55.1 2.9 %copy-start.3 = (bf16[48,3072]{1,0:T(8,128)(2,1)}, bf16[48,3072]{1,0:T(8,128)(2,1)S(1)}, u32[]{:S(2)}) copy-start(bf16[48,3072]{1,0:T(8,128)(2,1)S(1)} %get-tuple-element.76.a) | copy-start | bytes 884740
  55.1 10.1 %copy-start = (bf16[48,3072]{1,0:T(8,128)(2,1)}, bf16[48,3072]{1,0:T(8,128)(2,1)S(1)}, u32[]{:S(2)}) copy-start(bf16[48,3072]{1,0:T(8,128)(2,1)S(1)} %get-tuple-element.55.refs_0_) | copy-start | bytes 884740
  55.1 10.1 %copy-start.1 = (bf16[48,3072]{1,0:T(8,128)(2,1)}, bf16[48,3072]{1,0:T(8,128)(2,1)S(1)}, u32[]{:S(2)}) copy-start(bf16[48,3072]{1,0:T(8,128)(2,1)S(1)} %get-tuple-element.56.refs_1_) | copy-start | bytes 884740
  55.1 10.1 %copy-start.2 = (bf16[48,3072]{1,0:T(8,128)(2,1)}, bf16[48,3072]{1,0:T(8,128)(2,1)S(1)}, u32[]{:S(2)}) copy-start(bf16[48,3072]{1,0:T(8,128)(2,1)S(1)} %get-tuple-element.78.c) | copy-start | bytes 884740
  55.1 10.6 %collective-permute-start.14 = (bf16[48,3072]{1,0:T(8,128)(2,1)S(1)}, bf16[48,3072]{1,0:T(8,128)(2,1)S(1)}, u32[]{:S(2)}, u32[]{:S(2)}) collective-permute-start(bf16[48,3072]{1,0:T(8,128)(2,1)S(1)} %slice.14), channel_id=1, source_target_pairs={{0,8},{8,2},{2,10},{10,4},{4,12},{12,6},{6,14},{14,0},{1,9},{9,3},... | collective-permute-start | bytes 884744 | tf_op jit(solution)/shard_map/ppermute | solution.py:440
  55.3 10.5 %collective-permute-start.15 = (bf16[48,3072]{1,0:T(8,128)(2,1)S(1)}, bf16[48,3072]{1,0:T(8,128)(2,1)S(1)}, u32[]{:S(2)}, u32[]{:S(2)}) collective-permute-start(bf16[48,3072]{1,0:T(8,128)(2,1)S(1)} %slice.15), channel_id=1, source_target_pairs={{0,14},{8,0},{2,8},{10,2},{4,10},{12,4},{6,12},{14,6},{1,15},{9,1}... | collective-permute-start | bytes 884744 | tf_op jit(solution)/shard_map/ppermute | solution.py:440
  58.0 20.8 %collective-permute-start.9 = (bf16[12,144,128]{2,1,0:T(8,128)(2,1)S(1)}, bf16[12,144,128]{2,1,0:T(8,128)(2,1)S(1)}, u32[]{:S(2)}, u32[]{:S(2)}) collective-permute-start(bf16[12,144,128]{2,1,0:T(8,128)(2,1)S(1)} %bitcast.24), channel_id=1, source_target_pairs={{0,1},{1,0},{2,3},{3,2},{4,5},{5,4},{6,7},{7,6},{8,9},{9,8},{10,11... | collective-permute-start | bytes 1327112 | tf_op jit(solution)/shard_map/ppermute | solution.py:435
  65.2 14.3 %collective-permute-start.13 = (bf16[8,144,128]{2,1,0:T(8,128)(2,1)S(1)}, bf16[8,144,128]{2,1,0:T(8,128)(2,1)S(1)}, u32[]{:S(2)}, u32[]{:S(2)}) collective-permute-start(bf16[8,144,128]{2,1,0:T(8,128)(2,1)S(1)} %bitcast.26), channel_id=1, source_target_pairs={{0,1},{1,0},{2,3},{3,2},{4,5},{5,4},{6,7},{7,6},{8,9},{9,8},{10,11... | collective-permute-start | bytes 884744 | tf_op jit(solution)/shard_map/ppermute | solution.py:435
  65.3 14.2 %collective-permute-start.12 = (bf16[8,144,128]{2,1,0:T(8,128)(2,1)S(1)}, bf16[8,144,128]{2,1,0:T(8,128)(2,1)S(1)}, u32[]{:S(2)}, u32[]{:S(2)}) collective-permute-start(bf16[8,144,128]{2,1,0:T(8,128)(2,1)S(1)} %bitcast.25), channel_id=1, source_target_pairs={{0,1},{1,0},{2,3},{3,2},{4,5},{5,4},{6,7},{7,6},{8,9},{9,8},{10,11... | collective-permute-start | bytes 884744 | tf_op jit(solution)/shard_map/ppermute | solution.py:435
  74.9 17.9 %collective-permute-start.19 = (bf16[48,3072]{1,0:T(8,128)(2,1)}, bf16[48,3072]{1,0:T(8,128)(2,1)}, u32[]{:S(2)}, u32[]{:S(2)}) collective-permute-start(bf16[48,3072]{1,0:T(8,128)(2,1)} %get-tuple-element.77), channel_id=1, source_target_pairs={{0,2},{8,10},{2,4},{10,12},{4,6},{12,14},{6,0},{14,8},{1,3},{9,11}... | collective-permute-start | bytes 884744 | tf_op jit(solution)/shard_map/ppermute | solution.py:440
  75.8 17.6 %collective-permute-start.20 = (bf16[48,3072]{1,0:T(8,128)(2,1)S(1)}, bf16[48,3072]{1,0:T(8,128)(2,1)}, u32[]{:S(2)}, u32[]{:S(2)}) collective-permute-start(bf16[48,3072]{1,0:T(8,128)(2,1)S(1)} %get-tuple-element.79), channel_id=1, source_target_pairs={{0,6},{8,14},{2,0},{10,8},{4,2},{12,10},{6,4},{14,12},{1,7},{9,15}... | collective-permute-start | bytes 884744 | tf_op jit(solution)/shard_map/ppermute | solution.py:440
  78.8 1.6 %collective-permute-start.16 = (bf16[4,144,128]{2,1,0:T(8,128)(2,1)S(1)}, bf16[4,144,128]{2,1,0:T(8,128)(2,1)S(1)}, u32[]{:S(2)}, u32[]{:S(2)}) collective-permute-start(bf16[4,144,128]{2,1,0:T(8,128)(2,1)S(1)} %bitcast.27), channel_id=1, source_target_pairs={{0,1},{1,0},{2,3},{3,2},{4,5},{5,4},{6,7},{7,6},{8,9},{9,8},{10,11... | collective-permute-start | bytes 442376 | tf_op jit(solution)/shard_map/ppermute | solution.py:435
  83.6 38.7 %all-to-all-start = ((bf16[64,144,128]{2,1,0:T(8,128)(2,1)}), bf16[64,144,128]{2,1,0:T(8,128)(2,1)S(1)}, u32[]{:S(2)}, u32[]{:S(2)}) async-start(bf16[64,144,128]{2,1,0:T(8,128)(2,1)} %pack.1), calls=%async_computation | async-start | bytes 4718592 | tf_op jit(solution)/shard_map/all_to_all | solution.py:494
  90.4 11.5 %collective-permute-start.17 = (bf16[48,3072]{1,0:T(8,128)(2,1)S(1)}, bf16[48,3072]{1,0:T(8,128)(2,1)S(1)}, u32[]{:S(2)}, u32[]{:S(2)}) collective-permute-start(bf16[48,3072]{1,0:T(8,128)(2,1)S(1)} %get-tuple-element.74), channel_id=1, source_target_pairs={{0,6},{8,14},{2,0},{10,8},{4,2},{12,10},{6,4},{14,12},{1,7},{9,15}... | collective-permute-start | bytes 884744 | tf_op jit(solution)/shard_map/ppermute | solution.py:440
  91.0 11.2 %collective-permute-start.18 = (bf16[48,3072]{1,0:T(8,128)(2,1)S(1)}, bf16[48,3072]{1,0:T(8,128)(2,1)}, u32[]{:S(2)}, u32[]{:S(2)}) collective-permute-start(bf16[48,3072]{1,0:T(8,128)(2,1)S(1)} %get-tuple-element.75), channel_id=1, source_target_pairs={{0,2},{8,10},{2,4},{10,12},{4,6},{12,14},{6,0},{14,8},{1,3},{9,11}... | collective-permute-start | bytes 884744 | tf_op jit(solution)/shard_map/ppermute | solution.py:440
  95.5 15.0 %collective-permute-start.21 = (bf16[48,3072]{1,0:T(8,128)(2,1)}, bf16[48,3072]{1,0:T(8,128)(2,1)S(1)}, u32[]{:S(2)}, u32[]{:S(2)}) collective-permute-start(bf16[48,3072]{1,0:T(8,128)(2,1)} %get-tuple-element.80), channel_id=1, source_target_pairs={{0,2},{8,10},{2,4},{10,12},{4,6},{12,14},{6,0},{14,8},{1,3},{9,11}... | collective-permute-start | bytes 884744 | tf_op jit(solution)/shard_map/ppermute | solution.py:440
  97.0 15.3 %collective-permute-start.22 = (bf16[48,3072]{1,0:T(8,128)(2,1)}, bf16[48,3072]{1,0:T(8,128)(2,1)}, u32[]{:S(2)}, u32[]{:S(2)}) collective-permute-start(bf16[48,3072]{1,0:T(8,128)(2,1)} %get-tuple-element.81), channel_id=1, source_target_pairs={{0,6},{8,14},{2,0},{10,8},{4,2},{12,10},{6,4},{14,12},{1,7},{9,15}... | collective-permute-start | bytes 884744 | tf_op jit(solution)/shard_map/ppermute | solution.py:440
  101.9 10.4 %copy-start.4 = (bf16[48,3072]{1,0:T(8,128)(2,1)}, bf16[48,3072]{1,0:T(8,128)(2,1)S(1)}, u32[]{:S(2)}) copy-start(bf16[48,3072]{1,0:T(8,128)(2,1)S(1)} %collective-permute-done.17.refs_2_) | copy-start | bytes 884740
  110.4 1.8 %copy-start.5 = (bf16[48,3072]{1,0:T(8,128)(2,1)}, bf16[48,3072]{1,0:T(8,128)(2,1)S(1)}, u32[]{:S(2)}) copy-start(bf16[48,3072]{1,0:T(8,128)(2,1)S(1)} %collective-permute-done.21.refs_4_) | copy-start | bytes 884740

commit v2 on v1

--- a/solution.py
+++ b/solution.py
@@ -325,6 +325,52 @@
     return res[:-2], wire[0], wire[1]
 
 
+def attn_kernel(backs, *refs):
+    meta, lens, cosine, sine = refs[:4]
+    weights, (x, k, v), (wq_v, wo_v), outs = refs[4:8], refs[8:11], refs[11:13], refs[13:15]
+    cos_scr, sin_scr, x_scr, k_scr, v_scr, attn_scr, part_scr, small, rest_sem = refs[15:]
+    per_dev = wq_v.shape[2]
+    firsts = ((x, x_scr), (cosine, cos_scr), (sine, sin_scr), (k, k_scr), (v, v_scr))
+    for i, (src, dst) in enumerate(firsts):
+        load(src, dst, small.at[i])
+    load_rest(weights, wq_v, wo_v, rest_sem)
+    masks = score_masks(backs, meta, lens, per_dev // HD)
+    for i, (src, dst) in enumerate(firsts):
+        landed(dst, small.at[i])
+
+    def body(shard, carry):
+        landed(wq_v.at[shard], rest_sem.at[shard])
+        attend_shard(shard, masks, x_scr, k_scr, v_scr, wq_v, cos_scr[...], sin_scr[...], attn_scr)
+        return carry
+
+    lax.fori_loop(0, 2, body, 0)
+    rest_landed(wo_v, per_dev, rest_sem)
+    project(attn_scr, wo_v, part_scr, outs, small)
+    for i, out in enumerate(outs):
+        landed(out, small.at[i])
+
+
+def attn_call(backs, meta, lens, tables, weights, kept):
+    width, per_dev = weights[0].shape
+    scr = lambda *shape: pltpu.VMEM(shape, jnp.bfloat16)
+    dma = pltpu.SemaphoreType.DMA
+    return pl.pallas_call(
+        functools.partial(attn_kernel, backs),
+        out_shape=held_shapes(width, per_dev)[1:] + [jax.ShapeDtypeStruct((HALF, width), jnp.bfloat16)] * 2,
+        in_specs=[SMEM, SMEM] + [HBM] * 9,
+        out_specs=[VMEM] * 2 + [HBM] * 2,
+        scratch_shapes=[pltpu.VMEM(y.shape, y.dtype) for y in tables]
+        + [scr(*y.shape) for y in kept]
+        + [scr(ROWS, 2 * per_dev), scr(ROWS, width)]
+        + [dma((5,)), dma((4,))],
+        compiler_params=pltpu.CompilerParams(vmem_limit_bytes=24 << 20),
+        cost_estimate=pl.CostEstimate(
+            flops=ROWS * width * per_dev // 4, bytes_accessed=1 << 18, transcendentals=0
+        ),
+        name="attend",
+    )(meta, lens, *pinned(tables, pltpu.HBM), *weights, *kept)
+
+
 def pack_kernel(order, meta, slots, empty, *refs):
     sources = refs[: len(order)]
     out, *wires, blank, sem, in_sem = refs[len(order) :]
@@ -421,11 +467,15 @@
 
 
 def finish_call(flat, terms):
+    rows, width = flat.shape
+    step = width // 4
+    block = lambda n: pl.BlockSpec((n, step), lambda c: (0, c))
     return pl.pallas_call(
         finish_kernel,
         out_shape=jax.ShapeDtypeStruct(flat.shape, flat.dtype),
-        in_specs=[VMEM] * (1 + len(terms)),
-        out_specs=VMEM,
+        grid=(4,),
+        in_specs=[block(rows)] + [block(HALF)] * len(terms),
+        out_specs=block(rows),
         cost_estimate=pl.CostEstimate(flops=flat.size, bytes_accessed=1 << 18, transcendentals=0),
         name="finish",
     )(flat, *terms)
@@ -478,11 +528,11 @@
     rest = (*pinned((w_q,), pltpu.HBM), swap(wq_late, "core"), *pinned((w_o,), pltpu.HBM), swap(wo_late, "core"))
     first = (*pinned((w_k, w_v), pltpu.HBM), wk_p, wv_p)
     (held, *kept), done = keys((0, 1, -1), (), 1, first, (), (*pinned((flat,), pltpu.HBM), u1, d1))
-    u2, d2, done = bar((u2, d2, done))
+    *held_rest, top0, bottom0 = attn_call((0,), meta, lens, tables[1:], rest, kept)
+    u2, d2, done, top0 = bar((u2, d2, done, top0))
     wires[0] = done
     u3, d3 = shift(u2, 1), shift(d2, -1)
-    extra, done = keys((2, -2), (2, -2, 0), 0, (held,), rest, (u2, d2), kept)
-    held_rest, (top1, bottom1, top2, bottom2, *part0) = extra[:2], extra[2:]
+    (top1, bottom1, top2, bottom2), done = keys((2, -2), (2, -2), 0, (held,), held_rest, (u2, d2))
     u3, d3, done = bar((u3, d3, done))
     wires[2] = done
     far = shift(u3[:HALF], 1), shift(d3[HALF:], -1)
@@ -496,7 +546,7 @@
     near_t, near_b = shift(top1, -2), shift(bottom2, 2)
     top2, bottom1 = merge_call(top2, passing_t, bottom1, passing_b)
     merged_t, merged_b = shift(top2, 2), shift(bottom1, -2)
-    terms = (*part0, near_t, near_b, merged_t, merged_b)
+    terms = (top0, bottom0, near_t, near_b, merged_t, merged_b)
     hidden_out = finish_call(flat, terms).reshape(hidden_in.shape)
     return hidden_out, place_call(inbound, per_dev)
 

time: 125 us -> 129 us (1.032)
  Pallas kernels: 45.1 us -> 50.2 us
  starting transfers between devices: 37.5 us -> 40.5 us
  waiting for transfers between devices: 36.3 us -> 33.9 us
  other arithmetic: 3.64 us -> 1.97 us
    all_to_all x1, waiting for transfers between devices: 7.39 us -> 0.01 us  [on_device(): lax.all_to_all(outbound, 'xy', split_axis=0, concat_axis=0, tiled=True)]
    pallas_call x0 -> x1, Pallas kernels: none -> 6.93 us  [attn_call(): pl.pallas_call(functools.partial(attn_kernel, backs), out_shape=held_shap...]
    ppermute x9, starting transfers between devices: 5.78 us -> 9.49 us  [swap(): return lax.ppermute(x, axis, [(0, 1), (1, 0)])]
    pallas_call x4, Pallas kernels: 35.8 us -> 32.9 us  [kv_call(): pl.pallas_call(functools.partial(kv_kernel, backs, att, keep, len(chunks)...]
    ppermute x9, waiting for transfers between devices: 7.9 us -> 10.6 us  [swap(): return lax.ppermute(x, axis, [(0, 1), (1, 0)])]
    ppermute x14, waiting for transfers between devices: 21 us -> 23.3 us  [shift(): lax.ppermute(x, ('zl', 'zh'), [(at(z), at((z + by) % NZ)) for z in range(...]
  transfers between devices with their start and end apart: 24 -> 24, of which waited for: 11 -> 7; matrix products, arithmetic and copies ran while one was open for 3% -> 2% of each run, Pallas kernels for 35% -> 38%
where the time goes in v2:
time: 129 us
  Pallas kernels  50.2 us (39%)
  starting transfers between devices  40.5 us (31%)
  waiting for transfers between devices  33.9 us (26%)
  other arithmetic  1.97 us (2%)
    pallas_call x4, Pallas kernels, kv_call(): pl.pallas_call(functools.partial(kv_kernel, backs, att, keep, len(chunks)...  32.9 us
    ppermute x14, starting transfers between devices, shift(): lax.ppermute(x, ('zl', 'zh'), [(at(z), at((z + by) % NZ)) for z in range(...  24.3 us
    ppermute x14, waiting for transfers between devices, shift(): lax.ppermute(x, ('zl', 'zh'), [(at(z), at((z + by) % NZ)) for z in range(...  23.3 us
    ppermute x9, waiting for transfers between devices, swap(): return lax.ppermute(x, axis, [(0, 1), (1, 0)])  10.6 us
    ppermute x9, starting transfers between devices, swap(): return lax.ppermute(x, axis, [(0, 1), (1, 0)])  9.49 us
    pallas_call x1, Pallas kernels, attn_call(): pl.pallas_call(functools.partial(attn_kernel, backs), out_shape=held_shap...  6.93 us
    all_to_all x1, starting transfers between devices, on_device(): lax.all_to_all(outbound, 'xy', split_axis=0, concat_axis=0, tiled=True)  6.76 us
    pallas_call x1, Pallas kernels, finish_call(): pl.pallas_call(finish_kernel, out_shape=jax.ShapeDtypeStruct(flat.shape,...  3.71 us
  transfers between devices with their start and end apart: 24, of which 7 were waited for; matrix products, arithmetic and copies ran while one was open for 2% of the time, Pallas kernels for 38%

profile of v2, /device:TPU:1, one launch (start us, length us, event | category | flops | bytes accessed | tf_op | source)
XLA Modules:
  0.0 128.6 jit_solution(5443848028216630374)
XLA Ops:
  0.6 6.5 %collective-permute-start.1 = (bf16[96,3072]{1,0:T(8,128)(2,1)}, bf16[96,3072]{1,0:T(8,128)(2,1)S(1)}, u32[]{:S(2)}, u32[]{:S(2)}) collective-permute-start(bf16[96,3072]{1,0:T(8,128)(2,1)} %bitcast.28), channel_id=1, source_target_pairs={{0,14},{8,0},{2,8},{10,2},{4,10},{12,4},{6,12},{14,6},{1,15},{9,1}... | collective-permute-start | bytes 1769480 | tf_op jit(solution)/shard_map/ppermute | solution.py:490
  7.1 0.7 pad_add_fusion.1
  7.9 0.0 collective-permute-start.2
  7.9 1.0 collective-permute-start.5
  8.9 0.1 collective-permute-start.6
  9.0 0.7 fusion.1
  9.8 0.1 pad_add_fusion.refs_0_.meta
  9.9 9.6 %collective-permute-done.2 = s32[64]{0:T(128)S(1)} collective-permute-done((s32[64]{0:T(128)S(1)}, s32[64]{0:T(128)S(1)}, u32[]{:S(2)}, u32[]{:S(2)}) %collective-permute-start.2) | collective-permute-done | bytes 288 | tf_op jit(solution)/shard_map/ppermute | solution.py:485
  19.5 0.1 slice.13
  19.5 0.2 convert_reduce_fusion
  19.7 0.1 compare_select_fusion
  19.8 0.1 reshape.68.slots
  19.9 0.1 fusion
  20.0 0.1 reshape.67.refs_1_
  20.1 2.4 %collective-permute-done.refs_10_ = bf16[96,3072]{1,0:T(8,128)(2,1)} collective-permute-done((bf16[96,3072]{1,0:T(8,128)(2,1)}, bf16[96,3072]{1,0:T(8,128)(2,1)}, u32[]{:S(2)}, u32[]{:S(2)}) %collective-permute-start) | collective-permute-done | bytes 589856 | tf_op jit(solution)/shard_map/ppermute | solution.py:490
  22.5 1.9 %collective-permute-start.7 = (bf16[3072,384]{1,0:T(8,128)(2,1)}, bf16[3072,384]{1,0:T(8,128)(2,1)S(1)}, u32[]{:S(2)}, u32[]{:S(2)}) collective-permute-start(bf16[3072,384]{1,0:T(8,128)(2,1)} %refs_4_.5), channel_id=1, source_target_pairs={{0,1},{1,0},{2,3},{3,2},{4,5},{5,4},{6,7},{7,6},{8,9},{9,8},{10,11... | collective-permute-start | bytes 7077896 | tf_op jit(solution)/shard_map/ppermute | solution.py:485
  24.4 0.0 collective-permute-start.8
  24.4 2.7 %collective-permute-start.4 = (bf16[96,3072]{1,0:T(8,128)(2,1)S(1)}, bf16[96,3072]{1,0:T(8,128)(2,1)S(1)}, u32[]{:S(2)}, u32[]{:S(2)}) collective-permute-start(bf16[96,3072]{1,0:T(8,128)(2,1)S(1)} %collective-permute-done.1.refs_11_), channel_id=1, source_target_pairs={{0,14},{8,0},{2,8},{10,2},{4,10},{12,4},{6,12},{14,6},{1,15},{9,1}... | collective-permute-start | bytes 1769480 | tf_op jit(solution)/shard_map/ppermute | solution.py:490
  27.1 7.9 %keys.4 = (bf16[2,3072,768]{2,1,0:T(8,128)(2,1)S(1)}, bf16[96,3072]{1,0:T(8,128)(2,1)S(1)}, bf16[96,768]{1,0:T(8,128)(2,1)S(1)}, bf16[96,768]{1,0:T(8,128)(2,1)S...) custom-call(s32[2]{0:T(128)S(1)} %pad_add_fusion.refs_0_.meta, s32[64]{0:T(128)S(1)} %reshape.67.refs_1_, ...), custom_call_target="tpu_custom_call" | custom-call | flops 84934656 | bytes 262144 | tf_op jit(solution)/shard_map/keys/pallas_call | solution.py:308
  35.0 6.9 %attend.1 = (bf16[2,3072,384]{2,1,0:T(8,128)(2,1)S(1)}, bf16[768,3072]{1,0:T(8,128)(2,1)S(1)}, bf16[48,3072]{1,0:T(8,128)(2,1)S(1)}, bf16[48,3072]{1,0:T(8,128)(2,1)S(1)}) custom-call(s32[2]{0:T(128)S(1)} %pad_add_fusion.refs_0_.meta, s32[64]{0:T(128)S(1)} %reshape.67.refs_1_, f32[24,384]{1,0:T(8,128)} %constant.49.clone.refs_3_.refs_2_, ...), custom_call_target="tpu_custom_call" | custom-call | flops 28311552 | bytes 262144 | tf_op jit(solution)/shard_map/attend/pallas_call | solution.py:357
  42.0 0.1 collective-permute-start.10
  42.1 2.7 %collective-permute-start.11 = (bf16[96,3072]{1,0:T(8,128)(2,1)S(1)}, bf16[96,3072]{1,0:T(8,128)(2,1)S(1)}, u32[]{:S(2)}, u32[]{:S(2)}) collective-permute-start(bf16[96,3072]{1,0:T(8,128)(2,1)S(1)} %collective-permute-done.4.refs_9_), channel_id=1, source_target_pairs={{0,14},{8,0},{2,8},{10,2},{4,10},{12,4},{6,12},{14,6},{1,15},{9,1}... | collective-permute-start | bytes 1769480 | tf_op jit(solution)/shard_map/ppermute | solution.py:490
  44.8 11.2 %keys.5 = (bf16[48,3072]{1,0:T(8,128)(2,1)S(1)}, bf16[48,3072]{1,0:T(8,128)(2,1)S(1)}, bf16[48,3072]{1,0:T(8,128)(2,1)S(1)}, bf16[48,3072]{1,0:T(8,128)(2,1)S(1)...) custom-call(s32[2]{0:T(128)S(1)} %pad_add_fusion.refs_0_.meta, s32[64]{0:T(128)S(1)} %reshape.67.refs_1_, ...), custom_call_target="tpu_custom_call" | custom-call | flops 113246208 | bytes 262144 | tf_op jit(solution)/shard_map/keys/pallas_call | solution.py:308
  56.0 0.0 copy-start.3
  56.0 1.0 collective-permute-done.10.refs_6_
  57.1 2.5 %collective-permute-start.15 = (bf16[48,3072]{1,0:T(8,128)(2,1)S(1)}, bf16[48,3072]{1,0:T(8,128)(2,1)S(1)}, u32[]{:S(2)}, u32[]{:S(2)}) collective-permute-start(bf16[48,3072]{1,0:T(8,128)(2,1)S(1)} %slice.15), channel_id=1, source_target_pairs={{0,14},{8,0},{2,8},{10,2},{4,10},{12,4},{6,12},{14,6},{1,15},{9,1}... | collective-permute-start | bytes 884744 | tf_op jit(solution)/shard_map/ppermute | solution.py:490
  59.6 2.5 %collective-permute-start.9 = (bf16[12,144,128]{2,1,0:T(8,128)(2,1)S(1)}, bf16[12,144,128]{2,1,0:T(8,128)(2,1)S(1)}, u32[]{:S(2)}, u32[]{:S(2)}) collective-permute-start(bf16[12,144,128]{2,1,0:T(8,128)(2,1)S(1)} %bitcast.24), channel_id=1, source_target_pairs={{0,1},{1,0},{2,3},{3,2},{4,5},{5,4},{6,7},{7,6},{8,9},{9,8},{10,11... | collective-permute-start | bytes 1327112 | tf_op jit(solution)/shard_map/ppermute | solution.py:485
  62.2 0.0 collective-permute-start.12
  62.2 4.7 %keys.6 = (bf16[1152,128]{1,0:T(8,128)(2,1)S(1)}, bf16[1152,128]{1,0:T(8,128)(2,1)S(1)}) custom-call(s32[2]{0:T(128)S(1)} %pad_add_fusion.refs_0_.meta, s32[64]{0:T(128)S(1)} %reshape.67.refs_1_, f32[1,3072]{1,0:T(1,128)} %bitcast.35, f32[24,384]{1,0:T(8,128)} %constant.49.clone.refs_3_.refs_2_, f32[24,384]{1,0:T(8,128)} %constant.50.clone.refs_4_.refs_3_, ...), custom_call_target="tpu_custom_call" | custom-call | flops 56623104 | bytes 262144 | tf_op jit(solution)/shard_map/keys/pallas_call | solution.py:308
  66.9 0.6 collective-permute-start.13
  67.5 9.1 %keys.7 = (bf16[48,3072]{1,0:T(8,128)(2,1)}, bf16[48,3072]{1,0:T(8,128)(2,1)S(1)}, bf16[576,128]{1,0:T(8,128)(2,1)S(1)}, bf16[576,128]{1,0:T(8,128)(2,1)S(1)}) custom-call(s32[2]{0:T(128)S(1)} %pad_add_fusion.refs_0_.meta, s32[64]{0:T(128)S(1)} %reshape.67.refs_1_, f32[1,3072]{1,0:T(1,128)} %bitcast.36, f32[24,384]{1,0:T(8,128)} %constant.49.clone.refs_3_.refs_2_, ...), custom_call_target="tpu_custom_call" | custom-call | flops 56623104 | bytes 262144 | tf_op jit(solution)/shard_map/keys/pallas_call | solution.py:308
  76.5 0.3 collective-permute-start.19
  76.9 3.6 %collective-permute-start.20 = (bf16[48,3072]{1,0:T(8,128)(2,1)S(1)}, bf16[48,3072]{1,0:T(8,128)(2,1)}, u32[]{:S(2)}, u32[]{:S(2)}) collective-permute-start(bf16[48,3072]{1,0:T(8,128)(2,1)S(1)} %get-tuple-element.81), channel_id=1, source_target_pairs={{0,6},{8,14},{2,0},{10,8},{4,2},{12,10},{6,4},{14,12},{1,7},{9,15}... | collective-permute-start | bytes 884744 | tf_op jit(solution)/shard_map/ppermute | solution.py:490
  80.4 3.3 %collective-permute-start.16 = (bf16[4,144,128]{2,1,0:T(8,128)(2,1)S(1)}, bf16[4,144,128]{2,1,0:T(8,128)(2,1)S(1)}, u32[]{:S(2)}, u32[]{:S(2)}) collective-permute-start(bf16[4,144,128]{2,1,0:T(8,128)(2,1)S(1)} %bitcast.27), channel_id=1, source_target_pairs={{0,1},{1,0},{2,3},{3,2},{4,5},{5,4},{6,7},{7,6},{8,9},{9,8},{10,11... | collective-permute-start | bytes 442376 | tf_op jit(solution)/shard_map/ppermute | solution.py:485
  83.8 1.0 collective-permute-done.16.refs_7_
  84.8 3.1 %pack.1 = bf16[64,144,128]{2,1,0:T(8,128)(2,1)} custom-call(s32[2]{0:T(128)S(1)} %pad_add_fusion.refs_0_.meta, s32[64]{0:T(128)S(1)} %reshape.68.slots, s32[64]{0:T(128)S(1)} %convert_subtract_fusion.empty, bf16[12,144,128]{2,1,0:T(8,128)(2,1)S(1)} %bitcast.20, bf16[12,144,128]{2,1,0:T(8,128)(2,1)S(1)} %collective-permute-done.9.refs_1_, ...), custom_call_target="tpu_custom_call" | custom-call | bytes 262144 | tf_op jit(solution)/shard_map/pack/pallas_call | solution.py:403
  87.9 6.8 %all-to-all-start = ((bf16[64,144,128]{2,1,0:T(8,128)(2,1)}), bf16[64,144,128]{2,1,0:T(8,128)(2,1)S(1)}, u32[]{:S(2)}, u32[]{:S(2)}) async-start(bf16[64,144,128]{2,1,0:T(8,128)(2,1)} %pack.1), calls=%async_computation | async-start | bytes 4718592 | tf_op jit(solution)/shard_map/all_to_all | solution.py:544
  94.7 0.1 collective-permute-start.17
  94.7 2.4 %collective-permute-start.18 = (bf16[48,3072]{1,0:T(8,128)(2,1)S(1)}, bf16[48,3072]{1,0:T(8,128)(2,1)}, u32[]{:S(2)}, u32[]{:S(2)}) collective-permute-start(bf16[48,3072]{1,0:T(8,128)(2,1)S(1)} %get-tuple-element.77), channel_id=1, source_target_pairs={{0,2},{8,10},{2,4},{10,12},{4,6},{12,14},{6,0},{14,8},{1,3},{9,11}... | collective-permute-start | bytes 884744 | tf_op jit(solution)/shard_map/ppermute | solution.py:490
  97.1 2.1 %merge.1 = (bf16[48,3072]{1,0:T(8,128)(2,1)}, bf16[48,3072]{1,0:T(8,128)(2,1)}) custom-call(bf16[48,3072]{1,0:T(8,128)(2,1)} %copy-done.3, bf16[48,3072]{1,0:T(8,128)(2,1)} %collective-permute-done.19.b, bf16[48,3072]{1,0:T(8,128)(2,1)} %copy-done.2, bf16[48,3072]{1,0:T(8,128)(2,1)} %collective-permute-done.20.d), custom_call_target="tpu_custom_call" | custom-call | flops 30000001024 | bytes 262144 | tf_op jit(solution)/shard_map/merge/pallas_call | solution.py:449
  99.2 0.0 collective-permute-start.21
  99.2 3.6 %collective-permute-start.22 = (bf16[48,3072]{1,0:T(8,128)(2,1)}, bf16[48,3072]{1,0:T(8,128)(2,1)}, u32[]{:S(2)}, u32[]{:S(2)}) collective-permute-start(bf16[48,3072]{1,0:T(8,128)(2,1)} %get-tuple-element.83), channel_id=1, source_target_pairs={{0,6},{8,14},{2,0},{10,8},{4,2},{12,10},{6,4},{14,12},{1,7},{9,15}... | collective-permute-start | bytes 884744 | tf_op jit(solution)/shard_map/ppermute | solution.py:490
  102.8 13.1 %collective-permute-done.17.refs_2_ = bf16[48,3072]{1,0:T(8,128)(2,1)S(1)} collective-permute-done((bf16[48,3072]{1,0:T(8,128)(2,1)S(1)}, bf16[48,3072]{1,0:T(8,128)(2,1)S(1)}, u32[]{:S(2)}, u32[]{:S(2)}) %collective-permute-start.17) | collective-permute-done | bytes 294944 | tf_op jit(solution)/shard_map/ppermute | solution.py:490
  115.9 0.5 collective-permute-done.18.refs_3_
  116.4 6.2 %collective-permute-done.21.refs_4_ = bf16[48,3072]{1,0:T(8,128)(2,1)S(1)} collective-permute-done((bf16[48,3072]{1,0:T(8,128)(2,1)}, bf16[48,3072]{1,0:T(8,128)(2,1)S(1)}, u32[]{:S(2)}, u32[]{:S(2)}) %collective-permute-start.21) | collective-permute-done | bytes 294944 | tf_op jit(solution)/shard_map/ppermute | solution.py:490
  122.6 0.7 copy-done.5
  123.3 3.7 %finish.1 = bf16[96,3072]{1,0:T(8,128)(2,1)} custom-call(bf16[96,3072]{1,0:T(8,128)(2,1)} %bitcast.31, bf16[48,3072]{1,0:T(8,128)(2,1)} %copy-done, bf16[48,3072]{1,0:T(8,128)(2,1)} %copy-done.1, bf16[48,3072]{1,0:T(8,128)(2,1)} %copy-done.4, bf16[48,3072]{1,0:T(8,128)(2,1)} %collective-permute-done.18.refs_3_, bf16[48,3072]{1,0:T(8,128)(2,1)} %copy-done.5, ...), custom_call_target="tpu_custom_call" | custom-call | flops 294912 | bytes 262144 | tf_op jit(solution)/shard_map/finish/pallas_call | solution.py:473
  127.0 1.4 %place.1 = bf16[64,24,2,384]{3,2,1,0:T(2,128)(2,1)} custom-call(bf16[64,24,3,2,128]{4,3,2,1,0:T(2,128)(2,1)S(1)} %bitcast.19), custom_call_target="tpu_custom_call" | custom-call | tf_op jit(solution)/shard_map/place/pallas_call | solution.py:432
  (36 shorter events, 0.1 us)
Async XLA Ops:
  0.6 19.5 %collective-permute-start.1 = (bf16[96,3072]{1,0:T(8,128)(2,1)}, bf16[96,3072]{1,0:T(8,128)(2,1)S(1)}, u32[]{:S(2)}, u32[]{:S(2)}) collective-permute-start(bf16[96,3072]{1,0:T(8,128)(2,1)} %bitcast.28), channel_id=1, source_target_pairs={{0,14},{8,0},{2,8},{10,2},{4,10},{12,4},{6,12},{14,6},{1,15},{9,1}... | collective-permute-start | bytes 1769480 | tf_op jit(solution)/shard_map/ppermute | solution.py:490
  7.1 15.4 %collective-permute-start = (bf16[96,3072]{1,0:T(8,128)(2,1)}, bf16[96,3072]{1,0:T(8,128)(2,1)}, u32[]{:S(2)}, u32[]{:S(2)}) collective-permute-start(bf16[96,3072]{1,0:T(8,128)(2,1)} %bitcast.29), channel_id=1, source_target_pairs={{0,8},{8,2},{2,10},{10,4},{4,12},{12,6},{6,14},{14,0},{1,9},{9,3},... | collective-permute-start | bytes 1769480 | tf_op jit(solution)/shard_map/ppermute | solution.py:490
  7.9 11.6 %collective-permute-start.2 = (s32[64]{0:T(128)S(1)}, s32[64]{0:T(128)S(1)}, u32[]{:S(2)}, u32[]{:S(2)}) collective-permute-start(s32[64]{0:T(128)S(1)} %pad_add_fusion.1), channel_id=1, source_target_pairs={{0,8},{8,0},{1,9},{9,1},{2,10},{10,2},{3,11},{11,3},{4,12},{12,4},... | collective-permute-start | bytes 776 | tf_op jit(solution)/shard_map/ppermute | solution.py:485
  7.9 16.5 %collective-permute-start.5 = (bf16[3072,384]{1,0:T(8,128)(2,1)}, bf16[3072,384]{1,0:T(8,128)(2,1)S(1)}, u32[]{:S(2)}, u32[]{:S(2)}) collective-permute-start(bf16[3072,384]{1,0:T(8,128)(2,1)} %refs_5_.1), channel_id=1, source_target_pairs={{0,1},{1,0},{2,3},{3,2},{4,5},{5,4},{6,7},{7,6},{8,9},{9,8},{10,11... | collective-permute-start | bytes 7077896 | tf_op jit(solution)/shard_map/ppermute | solution.py:485
  8.9 18.1 %collective-permute-start.6 = (bf16[3072,384]{1,0:T(8,128)(2,1)}, bf16[3072,384]{1,0:T(8,128)(2,1)}, u32[]{:S(2)}, u32[]{:S(2)}) collective-permute-start(bf16[3072,384]{1,0:T(8,128)(2,1)} %refs_6_.2), channel_id=1, source_target_pairs={{0,1},{1,0},{2,3},{3,2},{4,5},{5,4},{6,7},{7,6},{8,9},{9,8},{10,11... | collective-permute-start | bytes 7077896 | tf_op jit(solution)/shard_map/ppermute | solution.py:485
  22.5 12.5 %collective-permute-start.7 = (bf16[3072,384]{1,0:T(8,128)(2,1)}, bf16[3072,384]{1,0:T(8,128)(2,1)S(1)}, u32[]{:S(2)}, u32[]{:S(2)}) collective-permute-start(bf16[3072,384]{1,0:T(8,128)(2,1)} %refs_4_.5), channel_id=1, source_target_pairs={{0,1},{1,0},{2,3},{3,2},{4,5},{5,4},{6,7},{7,6},{8,9},{9,8},{10,11... | collective-permute-start | bytes 7077896 | tf_op jit(solution)/shard_map/ppermute | solution.py:485
  24.4 10.7 %collective-permute-start.8 = (bf16[384,3072]{1,0:T(8,128)(2,1)}, bf16[384,3072]{1,0:T(8,128)(2,1)S(1)}, u32[]{:S(2)}, u32[]{:S(2)}) collective-permute-start(bf16[384,3072]{1,0:T(8,128)(2,1)} %refs_6_.3), channel_id=1, source_target_pairs={{0,1},{1,0},{2,3},{3,2},{4,5},{5,4},{6,7},{7,6},{8,9},{9,8},{10,11... | collective-permute-start | bytes 7077896 | tf_op jit(solution)/shard_map/ppermute | solution.py:485
  24.4 17.6 %collective-permute-start.3 = (bf16[96,3072]{1,0:T(8,128)(2,1)}, bf16[96,3072]{1,0:T(8,128)(2,1)S(1)}, u32[]{:S(2)}, u32[]{:S(2)}) collective-permute-start(bf16[96,3072]{1,0:T(8,128)(2,1)} %collective-permute-done.refs_10_), channel_id=1, source_target_pairs={{0,8},{8,2},{2,10},{10,4},{4,12},{12,6},{6,14},{14,0},{1,9},{9,3},... | collective-permute-start | bytes 1769480 | tf_op jit(solution)/shard_map/ppermute | solution.py:490
  24.4 17.6 %collective-permute-start.4 = (bf16[96,3072]{1,0:T(8,128)(2,1)S(1)}, bf16[96,3072]{1,0:T(8,128)(2,1)S(1)}, u32[]{:S(2)}, u32[]{:S(2)}) collective-permute-start(bf16[96,3072]{1,0:T(8,128)(2,1)S(1)} %collective-permute-done.1.refs_11_), channel_id=1, source_target_pairs={{0,14},{8,0},{2,8},{10,2},{4,10},{12,4},{6,12},{14,6},{1,15},{9,1}... | collective-permute-start | bytes 1769480 | tf_op jit(solution)/shard_map/ppermute | solution.py:490
  42.0 14.0 %copy-start = (bf16[48,3072]{1,0:T(8,128)(2,1)}, bf16[48,3072]{1,0:T(8,128)(2,1)S(1)}, u32[]{:S(2)}) copy-start(bf16[48,3072]{1,0:T(8,128)(2,1)S(1)} %get-tuple-element.54.refs_0_) | copy-start | bytes 884740
  42.0 14.0 %copy-start.1 = (bf16[48,3072]{1,0:T(8,128)(2,1)}, bf16[48,3072]{1,0:T(8,128)(2,1)S(1)}, u32[]{:S(2)}) copy-start(bf16[48,3072]{1,0:T(8,128)(2,1)S(1)} %get-tuple-element.55.refs_1_) | copy-start | bytes 884740
  42.0 15.0 %collective-permute-start.10 = (bf16[96,3072]{1,0:T(8,128)(2,1)S(1)}, bf16[96,3072]{1,0:T(8,128)(2,1)S(1)}, u32[]{:S(2)}, u32[]{:S(2)}) collective-permute-start(bf16[96,3072]{1,0:T(8,128)(2,1)S(1)} %collective-permute-done.3.refs_8_), channel_id=1, source_target_pairs={{0,8},{8,2},{2,10},{10,4},{4,12},{12,6},{6,14},{14,0},{1,9},{9,3},... | collective-permute-start | bytes 1769480 | tf_op jit(solution)/shard_map/ppermute | solution.py:490
  42.1 15.0 %collective-permute-start.11 = (bf16[96,3072]{1,0:T(8,128)(2,1)S(1)}, bf16[96,3072]{1,0:T(8,128)(2,1)S(1)}, u32[]{:S(2)}, u32[]{:S(2)}) collective-permute-start(bf16[96,3072]{1,0:T(8,128)(2,1)S(1)} %collective-permute-done.4.refs_9_), channel_id=1, source_target_pairs={{0,14},{8,0},{2,8},{10,2},{4,10},{12,4},{6,12},{14,6},{1,15},{9,1}... | collective-permute-start | bytes 1769480 | tf_op jit(solution)/shard_map/ppermute | solution.py:490
  56.0 1.1 copy-start.3
  56.0 10.8 %copy-start.2 = (bf16[48,3072]{1,0:T(8,128)(2,1)}, bf16[48,3072]{1,0:T(8,128)(2,1)S(1)}, u32[]{:S(2)}) copy-start(bf16[48,3072]{1,0:T(8,128)(2,1)S(1)} %get-tuple-element.80.c) | copy-start | bytes 884740
  57.1 10.3 %collective-permute-start.15 = (bf16[48,3072]{1,0:T(8,128)(2,1)S(1)}, bf16[48,3072]{1,0:T(8,128)(2,1)S(1)}, u32[]{:S(2)}, u32[]{:S(2)}) collective-permute-start(bf16[48,3072]{1,0:T(8,128)(2,1)S(1)} %slice.15), channel_id=1, source_target_pairs={{0,14},{8,0},{2,8},{10,2},{4,10},{12,4},{6,12},{14,6},{1,15},{9,1}... | collective-permute-start | bytes 884744 | tf_op jit(solution)/shard_map/ppermute | solution.py:490
  59.6 7.9 %collective-permute-start.14 = (bf16[48,3072]{1,0:T(8,128)(2,1)S(1)}, bf16[48,3072]{1,0:T(8,128)(2,1)S(1)}, u32[]{:S(2)}, u32[]{:S(2)}) collective-permute-start(bf16[48,3072]{1,0:T(8,128)(2,1)S(1)} %slice.14), channel_id=1, source_target_pairs={{0,8},{8,2},{2,10},{10,4},{4,12},{12,6},{6,14},{14,0},{1,9},{9,3},... | collective-permute-start | bytes 884744 | tf_op jit(solution)/shard_map/ppermute | solution.py:490
  59.6 20.8 %collective-permute-start.9 = (bf16[12,144,128]{2,1,0:T(8,128)(2,1)S(1)}, bf16[12,144,128]{2,1,0:T(8,128)(2,1)S(1)}, u32[]{:S(2)}, u32[]{:S(2)}) collective-permute-start(bf16[12,144,128]{2,1,0:T(8,128)(2,1)S(1)} %bitcast.24), channel_id=1, source_target_pairs={{0,1},{1,0},{2,3},{3,2},{4,5},{5,4},{6,7},{7,6},{8,9},{9,8},{10,11... | collective-permute-start | bytes 1327112 | tf_op jit(solution)/shard_map/ppermute | solution.py:485
  62.2 21.6 %collective-permute-start.12 = (bf16[8,144,128]{2,1,0:T(8,128)(2,1)S(1)}, bf16[8,144,128]{2,1,0:T(8,128)(2,1)S(1)}, u32[]{:S(2)}, u32[]{:S(2)}) collective-permute-start(bf16[8,144,128]{2,1,0:T(8,128)(2,1)S(1)} %bitcast.25), channel_id=1, source_target_pairs={{0,1},{1,0},{2,3},{3,2},{4,5},{5,4},{6,7},{7,6},{8,9},{9,8},{10,11... | collective-permute-start | bytes 884744 | tf_op jit(solution)/shard_map/ppermute | solution.py:485
  66.9 16.9 %collective-permute-start.13 = (bf16[8,144,128]{2,1,0:T(8,128)(2,1)S(1)}, bf16[8,144,128]{2,1,0:T(8,128)(2,1)S(1)}, u32[]{:S(2)}, u32[]{:S(2)}) collective-permute-start(bf16[8,144,128]{2,1,0:T(8,128)(2,1)S(1)} %bitcast.26), channel_id=1, source_target_pairs={{0,1},{1,0},{2,3},{3,2},{4,5},{5,4},{6,7},{7,6},{8,9},{9,8},{10,11... | collective-permute-start | bytes 884744 | tf_op jit(solution)/shard_map/ppermute | solution.py:485
  76.5 20.6 %collective-permute-start.19 = (bf16[48,3072]{1,0:T(8,128)(2,1)}, bf16[48,3072]{1,0:T(8,128)(2,1)}, u32[]{:S(2)}, u32[]{:S(2)}) collective-permute-start(bf16[48,3072]{1,0:T(8,128)(2,1)} %get-tuple-element.79), channel_id=1, source_target_pairs={{0,2},{8,10},{2,4},{10,12},{4,6},{12,14},{6,0},{14,8},{1,3},{9,11}... | collective-permute-start | bytes 884744 | tf_op jit(solution)/shard_map/ppermute | solution.py:490
  76.9 20.2 %collective-permute-start.20 = (bf16[48,3072]{1,0:T(8,128)(2,1)S(1)}, bf16[48,3072]{1,0:T(8,128)(2,1)}, u32[]{:S(2)}, u32[]{:S(2)}) collective-permute-start(bf16[48,3072]{1,0:T(8,128)(2,1)S(1)} %get-tuple-element.81), channel_id=1, source_target_pairs={{0,6},{8,14},{2,0},{10,8},{4,2},{12,10},{6,4},{14,12},{1,7},{9,15}... | collective-permute-start | bytes 884744 | tf_op jit(solution)/shard_map/ppermute | solution.py:490
  80.4 4.3 %collective-permute-start.16 = (bf16[4,144,128]{2,1,0:T(8,128)(2,1)S(1)}, bf16[4,144,128]{2,1,0:T(8,128)(2,1)S(1)}, u32[]{:S(2)}, u32[]{:S(2)}) collective-permute-start(bf16[4,144,128]{2,1,0:T(8,128)(2,1)S(1)} %bitcast.27), channel_id=1, source_target_pairs={{0,1},{1,0},{2,3},{3,2},{4,5},{5,4},{6,7},{7,6},{8,9},{9,8},{10,11... | collective-permute-start | bytes 442376 | tf_op jit(solution)/shard_map/ppermute | solution.py:485
  87.9 39.1 %all-to-all-start = ((bf16[64,144,128]{2,1,0:T(8,128)(2,1)}), bf16[64,144,128]{2,1,0:T(8,128)(2,1)S(1)}, u32[]{:S(2)}, u32[]{:S(2)}) async-start(bf16[64,144,128]{2,1,0:T(8,128)(2,1)} %pack.1), calls=%async_computation | async-start | bytes 4718592 | tf_op jit(solution)/shard_map/all_to_all | solution.py:544
  94.7 21.2 %collective-permute-start.17 = (bf16[48,3072]{1,0:T(8,128)(2,1)S(1)}, bf16[48,3072]{1,0:T(8,128)(2,1)S(1)}, u32[]{:S(2)}, u32[]{:S(2)}) collective-permute-start(bf16[48,3072]{1,0:T(8,128)(2,1)S(1)} %get-tuple-element.76), channel_id=1, source_target_pairs={{0,6},{8,14},{2,0},{10,8},{4,2},{12,10},{6,4},{14,12},{1,7},{9,15}... | collective-permute-start | bytes 884744 | tf_op jit(solution)/shard_map/ppermute | solution.py:490
  94.7 21.6 %collective-permute-start.18 = (bf16[48,3072]{1,0:T(8,128)(2,1)S(1)}, bf16[48,3072]{1,0:T(8,128)(2,1)}, u32[]{:S(2)}, u32[]{:S(2)}) collective-permute-start(bf16[48,3072]{1,0:T(8,128)(2,1)S(1)} %get-tuple-element.77), channel_id=1, source_target_pairs={{0,2},{8,10},{2,4},{10,12},{4,6},{12,14},{6,0},{14,8},{1,3},{9,11}... | collective-permute-start | bytes 884744 | tf_op jit(solution)/shard_map/ppermute | solution.py:490
  99.2 23.4 %collective-permute-start.21 = (bf16[48,3072]{1,0:T(8,128)(2,1)}, bf16[48,3072]{1,0:T(8,128)(2,1)S(1)}, u32[]{:S(2)}, u32[]{:S(2)}) collective-permute-start(bf16[48,3072]{1,0:T(8,128)(2,1)} %get-tuple-element.82), channel_id=1, source_target_pairs={{0,2},{8,10},{2,4},{10,12},{4,6},{12,14},{6,0},{14,8},{1,3},{9,11}... | collective-permute-start | bytes 884744 | tf_op jit(solution)/shard_map/ppermute | solution.py:490
  99.2 23.4 %collective-permute-start.22 = (bf16[48,3072]{1,0:T(8,128)(2,1)}, bf16[48,3072]{1,0:T(8,128)(2,1)}, u32[]{:S(2)}, u32[]{:S(2)}) collective-permute-start(bf16[48,3072]{1,0:T(8,128)(2,1)} %get-tuple-element.83), channel_id=1, source_target_pairs={{0,6},{8,14},{2,0},{10,8},{4,2},{12,10},{6,4},{14,12},{1,7},{9,15}... | collective-permute-start | bytes 884744 | tf_op jit(solution)/shard_map/ppermute | solution.py:490
  115.9 6.8 %copy-start.4 = (bf16[48,3072]{1,0:T(8,128)(2,1)}, bf16[48,3072]{1,0:T(8,128)(2,1)S(1)}, u32[]{:S(2)}) copy-start(bf16[48,3072]{1,0:T(8,128)(2,1)S(1)} %collective-permute-done.17.refs_2_) | copy-start | bytes 884740
  122.6 0.7 copy-start.5

commit v3 on v2

--- a/solution.py
+++ b/solution.py
@@ -467,15 +467,11 @@
 
 
 def finish_call(flat, terms):
-    rows, width = flat.shape
-    step = width // 4
-    block = lambda n: pl.BlockSpec((n, step), lambda c: (0, c))
     return pl.pallas_call(
         finish_kernel,
         out_shape=jax.ShapeDtypeStruct(flat.shape, flat.dtype),
-        grid=(4,),
-        in_specs=[block(rows)] + [block(HALF)] * len(terms),
-        out_specs=block(rows),
+        in_specs=[VMEM] * (1 + len(terms)),
+        out_specs=VMEM,
         cost_estimate=pl.CostEstimate(flops=flat.size, bytes_accessed=1 << 18, transcendentals=0),
         name="finish",
     )(flat, *terms)
@@ -521,9 +517,10 @@
         wires.append(swap(other, "core"))
         return extra, own
 
-    u1, d1 = shift(flat, 1), shift(flat, -1)
+    d1 = shift(flat, -1)
+    u1 = shift(flat, 1)
     wk_p, wv_p = swap(w_k, "core"), swap(w_v, "core")
-    u1, d1, meta, lens, slots, empty, wq_late, wo_late = bar((u1, d1, meta, lens, slots, empty, w_q, w_o))
+    d1, u1, meta, lens, slots, empty, wq_late, wo_late = bar((d1, u1, meta, lens, slots, empty, w_q, w_o))
     u2, d2 = shift(u1, 1), shift(d1, -1)
     rest = (*pinned((w_q,), pltpu.HBM), swap(wq_late, "core"), *pinned((w_o,), pltpu.HBM), swap(wo_late, "core"))
     first = (*pinned((w_k, w_v), pltpu.HBM), wk_p, wv_p)

time: 129 us -> 128 us (level)
    ppermute x14, waiting for transfers between devices: 23.3 us -> 25.6 us  [shift(): lax.ppermute(x, ('zl', 'zh'), [(at(z), at((z + by) % NZ)) for z in range(...]
    ppermute x9, waiting for transfers between devices: 10.6 us -> 8.87 us  [swap(): return lax.ppermute(x, axis, [(0, 1), (1, 0)])]
  transfers between devices with their start and end apart: 24 -> 24, of which waited for: 7 -> 7; matrix products, arithmetic and copies ran while one was open for 2% -> 2% of each run, Pallas kernels for 38% -> 37%
where the time goes in v3:
time: 128 us
  Pallas kernels  49.2 us (38%)
  starting transfers between devices  40.2 us (31%)
  waiting for transfers between devices  34.5 us (27%)
  other arithmetic  1.97 us (2%)
    pallas_call x4, Pallas kernels, kv_call(): pl.pallas_call(functools.partial(kv_kernel, backs, att, keep, len(chunks)...  32.9 us
    ppermute x14, waiting for transfers between devices, shift(): lax.ppermute(x, ('zl', 'zh'), [(at(z), at((z + by) % NZ)) for z in range(...  25.6 us
    ppermute x14, starting transfers between devices, shift(): lax.ppermute(x, ('zl', 'zh'), [(at(z), at((z + by) % NZ)) for z in range(...  24.6 us
    ppermute x9, waiting for transfers between devices, swap(): return lax.ppermute(x, axis, [(0, 1), (1, 0)])  8.87 us
    ppermute x9, starting transfers between devices, swap(): return lax.ppermute(x, axis, [(0, 1), (1, 0)])  8.85 us
    pallas_call x1, Pallas kernels, attn_call(): pl.pallas_call(functools.partial(attn_kernel, backs), out_shape=held_shap...  6.93 us
    all_to_all x1, starting transfers between devices, on_device(): lax.all_to_all(outbound, 'xy', split_axis=0, concat_axis=0, tiled=True)  6.78 us
    pallas_call x1, Pallas kernels, pack_call(): pl.pallas_call(functools.partial(pack_kernel, order), out_shape=pltpu.HBM...  3.13 us
  transfers between devices with their start and end apart: 24, of which 7 were waited for; matrix products, arithmetic and copies ran while one was open for 2% of the time, Pallas kernels for 37%

profile of v3, /device:TPU:1, one launch (start us, length us, event | category | flops | bytes accessed | tf_op | source)
XLA Modules:
  0.0 127.9 jit_solution(12209154777457638525)
XLA Ops:
  0.6 2.5 %collective-permute-start.1 = (bf16[96,3072]{1,0:T(8,128)(2,1)}, bf16[96,3072]{1,0:T(8,128)(2,1)S(1)}, u32[]{:S(2)}, u32[]{:S(2)}) collective-permute-start(bf16[96,3072]{1,0:T(8,128)(2,1)} %bitcast.28), channel_id=1, source_target_pairs={{0,8},{8,2},{2,10},{10,4},{4,12},{12,6},{6,14},{14,0},{1,9},{9,3},... | collective-permute-start | bytes 1769480 | tf_op jit(solution)/shard_map/ppermute | solution.py:486
  3.2 4.0 %collective-permute-start = (bf16[96,3072]{1,0:T(8,128)(2,1)}, bf16[96,3072]{1,0:T(8,128)(2,1)}, u32[]{:S(2)}, u32[]{:S(2)}) collective-permute-start(bf16[96,3072]{1,0:T(8,128)(2,1)} %bitcast.29), channel_id=1, source_target_pairs={{0,14},{8,0},{2,8},{10,2},{4,10},{12,4},{6,12},{14,6},{1,15},{9,1}... | collective-permute-start | bytes 1769480 | tf_op jit(solution)/shard_map/ppermute | solution.py:486
  7.2 0.7 pad_add_fusion.1
  7.9 0.0 collective-permute-start.2
  8.0 1.0 collective-permute-start.5
  9.0 0.1 collective-permute-start.6
  9.1 0.7 fusion.1
  9.9 0.1 pad_add_fusion.refs_0_.meta
  10.0 7.8 %collective-permute-done.2 = s32[64]{0:T(128)S(1)} collective-permute-done((s32[64]{0:T(128)S(1)}, s32[64]{0:T(128)S(1)}, u32[]{:S(2)}, u32[]{:S(2)}) %collective-permute-start.2) | collective-permute-done | bytes 288 | tf_op jit(solution)/shard_map/ppermute | solution.py:481
  17.8 0.1 slice.13
  17.9 0.2 convert_reduce_fusion
  18.1 0.1 compare_select_fusion
  18.2 0.1 reshape.68.slots
  18.2 0.1 fusion
  18.4 0.1 reshape.67.refs_1_
  18.5 1.9 %collective-permute-done.1.refs_10_ = bf16[96,3072]{1,0:T(8,128)(2,1)S(1)} collective-permute-done((bf16[96,3072]{1,0:T(8,128)(2,1)}, bf16[96,3072]{1,0:T(8,128)(2,1)S(1)}, u32[]{:S(2)}, u32[]{:S(2)}) %collective-permute-start.1) | collective-permute-done | bytes 589856 | tf_op jit(solution)/shard_map/ppermute | solution.py:486
  20.4 1.2 collective-permute-start.7
  21.6 0.0 collective-permute-start.8
  21.6 2.9 %collective-permute-start.4 = (bf16[96,3072]{1,0:T(8,128)(2,1)}, bf16[96,3072]{1,0:T(8,128)(2,1)S(1)}, u32[]{:S(2)}, u32[]{:S(2)}) collective-permute-start(bf16[96,3072]{1,0:T(8,128)(2,1)} %collective-permute-done.refs_11_), channel_id=1, source_target_pairs={{0,14},{8,0},{2,8},{10,2},{4,10},{12,4},{6,12},{14,6},{1,15},{9,1}... | collective-permute-start | bytes 1769480 | tf_op jit(solution)/shard_map/ppermute | solution.py:486
  24.6 7.9 %keys.4 = (bf16[2,3072,768]{2,1,0:T(8,128)(2,1)S(1)}, bf16[96,3072]{1,0:T(8,128)(2,1)S(1)}, bf16[96,768]{1,0:T(8,128)(2,1)S(1)}, bf16[96,768]{1,0:T(8,128)(2,1)S...) custom-call(s32[2]{0:T(128)S(1)} %pad_add_fusion.refs_0_.meta, s32[64]{0:T(128)S(1)} %reshape.67.refs_1_, ...), custom_call_target="tpu_custom_call" | custom-call | flops 84934656 | bytes 262144 | tf_op jit(solution)/shard_map/keys/pallas_call | solution.py:308
  32.5 6.9 %attend.1 = (bf16[2,3072,384]{2,1,0:T(8,128)(2,1)S(1)}, bf16[768,3072]{1,0:T(8,128)(2,1)S(1)}, bf16[48,3072]{1,0:T(8,128)(2,1)S(1)}, bf16[48,3072]{1,0:T(8,128)(2,1)S(1)}) custom-call(s32[2]{0:T(128)S(1)} %pad_add_fusion.refs_0_.meta, s32[64]{0:T(128)S(1)} %reshape.67.refs_1_, f32[24,384]{1,0:T(8,128)} %constant.49.clone.refs_3_.refs_2_, ...), custom_call_target="tpu_custom_call" | custom-call | flops 28311552 | bytes 262144 | tf_op jit(solution)/shard_map/attend/pallas_call | solution.py:357
  39.5 0.3 collective-permute-start.10
  39.8 2.5 %collective-permute-start.11 = (bf16[96,3072]{1,0:T(8,128)(2,1)S(1)}, bf16[96,3072]{1,0:T(8,128)(2,1)S(1)}, u32[]{:S(2)}, u32[]{:S(2)}) collective-permute-start(bf16[96,3072]{1,0:T(8,128)(2,1)S(1)} %collective-permute-done.4.refs_9_), channel_id=1, source_target_pairs={{0,14},{8,0},{2,8},{10,2},{4,10},{12,4},{6,12},{14,6},{1,15},{9,1}... | collective-permute-start | bytes 1769480 | tf_op jit(solution)/shard_map/ppermute | solution.py:486
  42.3 11.2 %keys.5 = (bf16[48,3072]{1,0:T(8,128)(2,1)S(1)}, bf16[48,3072]{1,0:T(8,128)(2,1)S(1)}, bf16[48,3072]{1,0:T(8,128)(2,1)S(1)}, bf16[48,3072]{1,0:T(8,128)(2,1)S(1)...) custom-call(s32[2]{0:T(128)S(1)} %pad_add_fusion.refs_0_.meta, s32[64]{0:T(128)S(1)} %reshape.67.refs_1_, ...), custom_call_target="tpu_custom_call" | custom-call | flops 113246208 | bytes 262144 | tf_op jit(solution)/shard_map/keys/pallas_call | solution.py:308
  53.5 0.0 copy-start.3
  53.5 1.3 %collective-permute-done.10.refs_6_ = bf16[96,3072]{1,0:T(8,128)(2,1)S(1)} collective-permute-done((bf16[96,3072]{1,0:T(8,128)(2,1)S(1)}, bf16[96,3072]{1,0:T(8,128)(2,1)S(1)}, u32[]{:S(2)}, u32[]{:S(2)}) %collective-permute-start.10) | collective-permute-done | bytes 589856 | tf_op jit(solution)/shard_map/ppermute | solution.py:486
  54.9 2.4 %collective-permute-start.15 = (bf16[48,3072]{1,0:T(8,128)(2,1)S(1)}, bf16[48,3072]{1,0:T(8,128)(2,1)S(1)}, u32[]{:S(2)}, u32[]{:S(2)}) collective-permute-start(bf16[48,3072]{1,0:T(8,128)(2,1)S(1)} %slice.15), channel_id=1, source_target_pairs={{0,14},{8,0},{2,8},{10,2},{4,10},{12,4},{6,12},{14,6},{1,15},{9,1}... | collective-permute-start | bytes 884744 | tf_op jit(solution)/shard_map/ppermute | solution.py:486
  57.4 2.3 %collective-permute-start.9 = (bf16[12,144,128]{2,1,0:T(8,128)(2,1)S(1)}, bf16[12,144,128]{2,1,0:T(8,128)(2,1)S(1)}, u32[]{:S(2)}, u32[]{:S(2)}) collective-permute-start(bf16[12,144,128]{2,1,0:T(8,128)(2,1)S(1)} %bitcast.24), channel_id=1, source_target_pairs={{0,1},{1,0},{2,3},{3,2},{4,5},{5,4},{6,7},{7,6},{8,9},{9,8},{10,11... | collective-permute-start | bytes 1327112 | tf_op jit(solution)/shard_map/ppermute | solution.py:481
  59.6 4.7 %keys.6 = (bf16[1152,128]{1,0:T(8,128)(2,1)S(1)}, bf16[1152,128]{1,0:T(8,128)(2,1)S(1)}) custom-call(s32[2]{0:T(128)S(1)} %pad_add_fusion.refs_0_.meta, s32[64]{0:T(128)S(1)} %reshape.67.refs_1_, f32[1,3072]{1,0:T(1,128)} %bitcast.35, f32[24,384]{1,0:T(8,128)} %constant.49.clone.refs_3_.refs_2_, f32[24,384]{1,0:T(8,128)} %constant.50.clone.refs_4_.refs_3_, ...), custom_call_target="tpu_custom_call" | custom-call | flops 56623104 | bytes 262144 | tf_op jit(solution)/shard_map/keys/pallas_call | solution.py:308
  64.4 0.6 collective-permute-start.13
  65.0 9.1 %keys.7 = (bf16[48,3072]{1,0:T(8,128)(2,1)}, bf16[48,3072]{1,0:T(8,128)(2,1)S(1)}, bf16[576,128]{1,0:T(8,128)(2,1)S(1)}, bf16[576,128]{1,0:T(8,128)(2,1)S(1)}) custom-call(s32[2]{0:T(128)S(1)} %pad_add_fusion.refs_0_.meta, s32[64]{0:T(128)S(1)} %reshape.67.refs_1_, f32[1,3072]{1,0:T(1,128)} %bitcast.36, f32[24,384]{1,0:T(8,128)} %constant.49.clone.refs_3_.refs_2_, ...), custom_call_target="tpu_custom_call" | custom-call | flops 56623104 | bytes 262144 | tf_op jit(solution)/shard_map/keys/pallas_call | solution.py:308
  74.0 2.5 %collective-permute-start.19 = (bf16[48,3072]{1,0:T(8,128)(2,1)}, bf16[48,3072]{1,0:T(8,128)(2,1)}, u32[]{:S(2)}, u32[]{:S(2)}) collective-permute-start(bf16[48,3072]{1,0:T(8,128)(2,1)} %get-tuple-element.79), channel_id=1, source_target_pairs={{0,2},{8,10},{2,4},{10,12},{4,6},{12,14},{6,0},{14,8},{1,3},{9,11}... | collective-permute-start | bytes 884744 | tf_op jit(solution)/shard_map/ppermute | solution.py:486
  76.5 1.4 %collective-permute-start.20 = (bf16[48,3072]{1,0:T(8,128)(2,1)S(1)}, bf16[48,3072]{1,0:T(8,128)(2,1)}, u32[]{:S(2)}, u32[]{:S(2)}) collective-permute-start(bf16[48,3072]{1,0:T(8,128)(2,1)S(1)} %get-tuple-element.81), channel_id=1, source_target_pairs={{0,6},{8,14},{2,0},{10,8},{4,2},{12,10},{6,4},{14,12},{1,7},{9,15}... | collective-permute-start | bytes 884744 | tf_op jit(solution)/shard_map/ppermute | solution.py:486
  77.9 3.6 %collective-permute-start.16 = (bf16[4,144,128]{2,1,0:T(8,128)(2,1)S(1)}, bf16[4,144,128]{2,1,0:T(8,128)(2,1)S(1)}, u32[]{:S(2)}, u32[]{:S(2)}) collective-permute-start(bf16[4,144,128]{2,1,0:T(8,128)(2,1)S(1)} %bitcast.27), channel_id=1, source_target_pairs={{0,1},{1,0},{2,3},{3,2},{4,5},{5,4},{6,7},{7,6},{8,9},{9,8},{10,11... | collective-permute-start | bytes 442376 | tf_op jit(solution)/shard_map/ppermute | solution.py:481
  81.5 1.0 collective-permute-done.16.refs_7_
  82.5 3.1 %pack.1 = bf16[64,144,128]{2,1,0:T(8,128)(2,1)} custom-call(s32[2]{0:T(128)S(1)} %pad_add_fusion.refs_0_.meta, s32[64]{0:T(128)S(1)} %reshape.68.slots, s32[64]{0:T(128)S(1)} %convert_subtract_fusion.empty, bf16[12,144,128]{2,1,0:T(8,128)(2,1)S(1)} %bitcast.20, bf16[12,144,128]{2,1,0:T(8,128)(2,1)S(1)} %collective-permute-done.9.refs_1_, ...), custom_call_target="tpu_custom_call" | custom-call | bytes 262144 | tf_op jit(solution)/shard_map/pack/pallas_call | solution.py:403
  85.6 6.8 %all-to-all-start = ((bf16[64,144,128]{2,1,0:T(8,128)(2,1)}), bf16[64,144,128]{2,1,0:T(8,128)(2,1)S(1)}, u32[]{:S(2)}, u32[]{:S(2)}) async-start(bf16[64,144,128]{2,1,0:T(8,128)(2,1)} %pack.1), calls=%async_computation | async-start | bytes 4718592 | tf_op jit(solution)/shard_map/all_to_all | solution.py:541
  92.4 0.6 collective-permute-start.17
  93.1 1.8 %collective-permute-start.18 = (bf16[48,3072]{1,0:T(8,128)(2,1)S(1)}, bf16[48,3072]{1,0:T(8,128)(2,1)}, u32[]{:S(2)}, u32[]{:S(2)}) collective-permute-start(bf16[48,3072]{1,0:T(8,128)(2,1)S(1)} %get-tuple-element.77), channel_id=1, source_target_pairs={{0,2},{8,10},{2,4},{10,12},{4,6},{12,14},{6,0},{14,8},{1,3},{9,11}... | collective-permute-start | bytes 884744 | tf_op jit(solution)/shard_map/ppermute | solution.py:486
  94.9 2.1 %merge.1 = (bf16[48,3072]{1,0:T(8,128)(2,1)}, bf16[48,3072]{1,0:T(8,128)(2,1)}) custom-call(bf16[48,3072]{1,0:T(8,128)(2,1)} %copy-done.3, bf16[48,3072]{1,0:T(8,128)(2,1)} %collective-permute-done.19.b, bf16[48,3072]{1,0:T(8,128)(2,1)} %copy-done.2, bf16[48,3072]{1,0:T(8,128)(2,1)} %collective-permute-done.20.d), custom_call_target="tpu_custom_call" | custom-call | flops 30000001024 | bytes 262144 | tf_op jit(solution)/shard_map/merge/pallas_call | solution.py:449
  97.0 2.0 %collective-permute-start.21 = (bf16[48,3072]{1,0:T(8,128)(2,1)}, bf16[48,3072]{1,0:T(8,128)(2,1)S(1)}, u32[]{:S(2)}, u32[]{:S(2)}) collective-permute-start(bf16[48,3072]{1,0:T(8,128)(2,1)} %get-tuple-element.82), channel_id=1, source_target_pairs={{0,2},{8,10},{2,4},{10,12},{4,6},{12,14},{6,0},{14,8},{1,3},{9,11}... | collective-permute-start | bytes 884744 | tf_op jit(solution)/shard_map/ppermute | solution.py:486
  99.0 1.5 %collective-permute-start.22 = (bf16[48,3072]{1,0:T(8,128)(2,1)}, bf16[48,3072]{1,0:T(8,128)(2,1)}, u32[]{:S(2)}, u32[]{:S(2)}) collective-permute-start(bf16[48,3072]{1,0:T(8,128)(2,1)} %get-tuple-element.83), channel_id=1, source_target_pairs={{0,6},{8,14},{2,0},{10,8},{4,2},{12,10},{6,4},{14,12},{1,7},{9,15}... | collective-permute-start | bytes 884744 | tf_op jit(solution)/shard_map/ppermute | solution.py:486
  100.6 14.3 %collective-permute-done.17.refs_2_ = bf16[48,3072]{1,0:T(8,128)(2,1)S(1)} collective-permute-done((bf16[48,3072]{1,0:T(8,128)(2,1)S(1)}, bf16[48,3072]{1,0:T(8,128)(2,1)S(1)}, u32[]{:S(2)}, u32[]{:S(2)}) %collective-permute-start.17) | collective-permute-done | bytes 294944 | tf_op jit(solution)/shard_map/ppermute | solution.py:486
  114.9 1.8 %collective-permute-done.18.refs_3_ = bf16[48,3072]{1,0:T(8,128)(2,1)} collective-permute-done((bf16[48,3072]{1,0:T(8,128)(2,1)S(1)}, bf16[48,3072]{1,0:T(8,128)(2,1)}, u32[]{:S(2)}, u32[]{:S(2)}) %collective-permute-start.18) | collective-permute-done | bytes 294944 | tf_op jit(solution)/shard_map/ppermute | solution.py:486
  116.7 6.2 %collective-permute-done.21.refs_4_ = bf16[48,3072]{1,0:T(8,128)(2,1)S(1)} collective-permute-done((bf16[48,3072]{1,0:T(8,128)(2,1)}, bf16[48,3072]{1,0:T(8,128)(2,1)S(1)}, u32[]{:S(2)}, u32[]{:S(2)}) %collective-permute-start.21) | collective-permute-done | bytes 294944 | tf_op jit(solution)/shard_map/ppermute | solution.py:486
  122.9 0.7 copy-done.5
  123.6 2.7 %finish.1 = bf16[96,3072]{1,0:T(8,128)(2,1)} custom-call(bf16[96,3072]{1,0:T(8,128)(2,1)} %bitcast.31, bf16[48,3072]{1,0:T(8,128)(2,1)} %copy-done, bf16[48,3072]{1,0:T(8,128)(2,1)} %copy-done.1, bf16[48,3072]{1,0:T(8,128)(2,1)} %copy-done.4, bf16[48,3072]{1,0:T(8,128)(2,1)} %collective-permute-done.18.refs_3_, bf16[48,3072]{1,0:T(8,128)(2,1)} %copy-done.5, ...), custom_call_target="tpu_custom_call" | custom-call | flops 294912 | bytes 262144 | tf_op jit(solution)/shard_map/finish/pallas_call | solution.py:470
  126.3 1.4 %place.1 = bf16[64,24,2,384]{3,2,1,0:T(2,128)(2,1)} custom-call(bf16[64,24,3,2,128]{4,3,2,1,0:T(2,128)(2,1)S(1)} %bitcast.19), custom_call_target="tpu_custom_call" | custom-call | tf_op jit(solution)/shard_map/place/pallas_call | solution.py:432
  (36 shorter events, 0.1 us)
Async XLA Ops:
  0.6 19.7 %collective-permute-start.1 = (bf16[96,3072]{1,0:T(8,128)(2,1)}, bf16[96,3072]{1,0:T(8,128)(2,1)S(1)}, u32[]{:S(2)}, u32[]{:S(2)}) collective-permute-start(bf16[96,3072]{1,0:T(8,128)(2,1)} %bitcast.28), channel_id=1, source_target_pairs={{0,8},{8,2},{2,10},{10,4},{4,12},{12,6},{6,14},{14,0},{1,9},{9,3},... | collective-permute-start | bytes 1769480 | tf_op jit(solution)/shard_map/ppermute | solution.py:486
  3.2 17.2 %collective-permute-start = (bf16[96,3072]{1,0:T(8,128)(2,1)}, bf16[96,3072]{1,0:T(8,128)(2,1)}, u32[]{:S(2)}, u32[]{:S(2)}) collective-permute-start(bf16[96,3072]{1,0:T(8,128)(2,1)} %bitcast.29), channel_id=1, source_target_pairs={{0,14},{8,0},{2,8},{10,2},{4,10},{12,4},{6,12},{14,6},{1,15},{9,1}... | collective-permute-start | bytes 1769480 | tf_op jit(solution)/shard_map/ppermute | solution.py:486
  7.9 9.9 %collective-permute-start.2 = (s32[64]{0:T(128)S(1)}, s32[64]{0:T(128)S(1)}, u32[]{:S(2)}, u32[]{:S(2)}) collective-permute-start(s32[64]{0:T(128)S(1)} %pad_add_fusion.1), channel_id=1, source_target_pairs={{0,8},{8,0},{1,9},{9,1},{2,10},{10,2},{3,11},{11,3},{4,12},{12,4},... | collective-permute-start | bytes 776 | tf_op jit(solution)/shard_map/ppermute | solution.py:481
  8.0 13.7 %collective-permute-start.5 = (bf16[3072,384]{1,0:T(8,128)(2,1)}, bf16[3072,384]{1,0:T(8,128)(2,1)S(1)}, u32[]{:S(2)}, u32[]{:S(2)}) collective-permute-start(bf16[3072,384]{1,0:T(8,128)(2,1)} %refs_5_.1), channel_id=1, source_target_pairs={{0,1},{1,0},{2,3},{3,2},{4,5},{5,4},{6,7},{7,6},{8,9},{9,8},{10,11... | collective-permute-start | bytes 7077896 | tf_op jit(solution)/shard_map/ppermute | solution.py:481
  9.0 15.6 %collective-permute-start.6 = (bf16[3072,384]{1,0:T(8,128)(2,1)}, bf16[3072,384]{1,0:T(8,128)(2,1)}, u32[]{:S(2)}, u32[]{:S(2)}) collective-permute-start(bf16[3072,384]{1,0:T(8,128)(2,1)} %refs_6_.2), channel_id=1, source_target_pairs={{0,1},{1,0},{2,3},{3,2},{4,5},{5,4},{6,7},{7,6},{8,9},{9,8},{10,11... | collective-permute-start | bytes 7077896 | tf_op jit(solution)/shard_map/ppermute | solution.py:481
  20.4 12.1 %collective-permute-start.7 = (bf16[3072,384]{1,0:T(8,128)(2,1)}, bf16[3072,384]{1,0:T(8,128)(2,1)S(1)}, u32[]{:S(2)}, u32[]{:S(2)}) collective-permute-start(bf16[3072,384]{1,0:T(8,128)(2,1)} %refs_4_.5), channel_id=1, source_target_pairs={{0,1},{1,0},{2,3},{3,2},{4,5},{5,4},{6,7},{7,6},{8,9},{9,8},{10,11... | collective-permute-start | bytes 7077896 | tf_op jit(solution)/shard_map/ppermute | solution.py:481
  21.6 10.9 %collective-permute-start.8 = (bf16[384,3072]{1,0:T(8,128)(2,1)}, bf16[384,3072]{1,0:T(8,128)(2,1)S(1)}, u32[]{:S(2)}, u32[]{:S(2)}) collective-permute-start(bf16[384,3072]{1,0:T(8,128)(2,1)} %refs_6_.3), channel_id=1, source_target_pairs={{0,1},{1,0},{2,3},{3,2},{4,5},{5,4},{6,7},{7,6},{8,9},{9,8},{10,11... | collective-permute-start | bytes 7077896 | tf_op jit(solution)/shard_map/ppermute | solution.py:481
  21.6 17.9 %collective-permute-start.3 = (bf16[96,3072]{1,0:T(8,128)(2,1)S(1)}, bf16[96,3072]{1,0:T(8,128)(2,1)S(1)}, u32[]{:S(2)}, u32[]{:S(2)}) collective-permute-start(bf16[96,3072]{1,0:T(8,128)(2,1)S(1)} %collective-permute-done.1.refs_10_), channel_id=1, source_target_pairs={{0,8},{8,2},{2,10},{10,4},{4,12},{12,6},{6,14},{14,0},{1,9},{9,3},... | collective-permute-start | bytes 1769480 | tf_op jit(solution)/shard_map/ppermute | solution.py:486
  21.6 17.9 %collective-permute-start.4 = (bf16[96,3072]{1,0:T(8,128)(2,1)}, bf16[96,3072]{1,0:T(8,128)(2,1)S(1)}, u32[]{:S(2)}, u32[]{:S(2)}) collective-permute-start(bf16[96,3072]{1,0:T(8,128)(2,1)} %collective-permute-done.refs_11_), channel_id=1, source_target_pairs={{0,14},{8,0},{2,8},{10,2},{4,10},{12,4},{6,12},{14,6},{1,15},{9,1}... | collective-permute-start | bytes 1769480 | tf_op jit(solution)/shard_map/ppermute | solution.py:486
  39.5 14.0 %copy-start = (bf16[48,3072]{1,0:T(8,128)(2,1)}, bf16[48,3072]{1,0:T(8,128)(2,1)S(1)}, u32[]{:S(2)}) copy-start(bf16[48,3072]{1,0:T(8,128)(2,1)S(1)} %get-tuple-element.54.refs_0_) | copy-start | bytes 884740
  39.5 14.0 %copy-start.1 = (bf16[48,3072]{1,0:T(8,128)(2,1)}, bf16[48,3072]{1,0:T(8,128)(2,1)S(1)}, u32[]{:S(2)}) copy-start(bf16[48,3072]{1,0:T(8,128)(2,1)S(1)} %get-tuple-element.55.refs_1_) | copy-start | bytes 884740
  39.5 15.3 %collective-permute-start.10 = (bf16[96,3072]{1,0:T(8,128)(2,1)S(1)}, bf16[96,3072]{1,0:T(8,128)(2,1)S(1)}, u32[]{:S(2)}, u32[]{:S(2)}) collective-permute-start(bf16[96,3072]{1,0:T(8,128)(2,1)S(1)} %collective-permute-done.3.refs_8_), channel_id=1, source_target_pairs={{0,8},{8,2},{2,10},{10,4},{4,12},{12,6},{6,14},{14,0},{1,9},{9,3},... | collective-permute-start | bytes 1769480 | tf_op jit(solution)/shard_map/ppermute | solution.py:486
  39.8 15.1 %collective-permute-start.11 = (bf16[96,3072]{1,0:T(8,128)(2,1)S(1)}, bf16[96,3072]{1,0:T(8,128)(2,1)S(1)}, u32[]{:S(2)}, u32[]{:S(2)}) collective-permute-start(bf16[96,3072]{1,0:T(8,128)(2,1)S(1)} %collective-permute-done.4.refs_9_), channel_id=1, source_target_pairs={{0,14},{8,0},{2,8},{10,2},{4,10},{12,4},{6,12},{14,6},{1,15},{9,1}... | collective-permute-start | bytes 1769480 | tf_op jit(solution)/shard_map/ppermute | solution.py:486
  53.5 1.4 %copy-start.3 = (bf16[48,3072]{1,0:T(8,128)(2,1)}, bf16[48,3072]{1,0:T(8,128)(2,1)S(1)}, u32[]{:S(2)}) copy-start(bf16[48,3072]{1,0:T(8,128)(2,1)S(1)} %get-tuple-element.78.a) | copy-start | bytes 884740
  53.5 10.8 %copy-start.2 = (bf16[48,3072]{1,0:T(8,128)(2,1)}, bf16[48,3072]{1,0:T(8,128)(2,1)S(1)}, u32[]{:S(2)}) copy-start(bf16[48,3072]{1,0:T(8,128)(2,1)S(1)} %get-tuple-element.80.c) | copy-start | bytes 884740
  54.9 10.0 %collective-permute-start.15 = (bf16[48,3072]{1,0:T(8,128)(2,1)S(1)}, bf16[48,3072]{1,0:T(8,128)(2,1)S(1)}, u32[]{:S(2)}, u32[]{:S(2)}) collective-permute-start(bf16[48,3072]{1,0:T(8,128)(2,1)S(1)} %slice.15), channel_id=1, source_target_pairs={{0,14},{8,0},{2,8},{10,2},{4,10},{12,4},{6,12},{14,6},{1,15},{9,1}... | collective-permute-start | bytes 884744 | tf_op jit(solution)/shard_map/ppermute | solution.py:486
  57.4 7.6 %collective-permute-start.14 = (bf16[48,3072]{1,0:T(8,128)(2,1)S(1)}, bf16[48,3072]{1,0:T(8,128)(2,1)S(1)}, u32[]{:S(2)}, u32[]{:S(2)}) collective-permute-start(bf16[48,3072]{1,0:T(8,128)(2,1)S(1)} %slice.14), channel_id=1, source_target_pairs={{0,8},{8,2},{2,10},{10,4},{4,12},{12,6},{6,14},{14,0},{1,9},{9,3},... | collective-permute-start | bytes 884744 | tf_op jit(solution)/shard_map/ppermute | solution.py:486
  57.4 20.6 %collective-permute-start.9 = (bf16[12,144,128]{2,1,0:T(8,128)(2,1)S(1)}, bf16[12,144,128]{2,1,0:T(8,128)(2,1)S(1)}, u32[]{:S(2)}, u32[]{:S(2)}) collective-permute-start(bf16[12,144,128]{2,1,0:T(8,128)(2,1)S(1)} %bitcast.24), channel_id=1, source_target_pairs={{0,1},{1,0},{2,3},{3,2},{4,5},{5,4},{6,7},{7,6},{8,9},{9,8},{10,11... | collective-permute-start | bytes 1327112 | tf_op jit(solution)/shard_map/ppermute | solution.py:481
  59.6 21.9 %collective-permute-start.12 = (bf16[8,144,128]{2,1,0:T(8,128)(2,1)S(1)}, bf16[8,144,128]{2,1,0:T(8,128)(2,1)S(1)}, u32[]{:S(2)}, u32[]{:S(2)}) collective-permute-start(bf16[8,144,128]{2,1,0:T(8,128)(2,1)S(1)} %bitcast.25), channel_id=1, source_target_pairs={{0,1},{1,0},{2,3},{3,2},{4,5},{5,4},{6,7},{7,6},{8,9},{9,8},{10,11... | collective-permute-start | bytes 884744 | tf_op jit(solution)/shard_map/ppermute | solution.py:481
  64.4 17.1 %collective-permute-start.13 = (bf16[8,144,128]{2,1,0:T(8,128)(2,1)S(1)}, bf16[8,144,128]{2,1,0:T(8,128)(2,1)S(1)}, u32[]{:S(2)}, u32[]{:S(2)}) collective-permute-start(bf16[8,144,128]{2,1,0:T(8,128)(2,1)S(1)} %bitcast.26), channel_id=1, source_target_pairs={{0,1},{1,0},{2,3},{3,2},{4,5},{5,4},{6,7},{7,6},{8,9},{9,8},{10,11... | collective-permute-start | bytes 884744 | tf_op jit(solution)/shard_map/ppermute | solution.py:481
  74.0 20.8 %collective-permute-start.19 = (bf16[48,3072]{1,0:T(8,128)(2,1)}, bf16[48,3072]{1,0:T(8,128)(2,1)}, u32[]{:S(2)}, u32[]{:S(2)}) collective-permute-start(bf16[48,3072]{1,0:T(8,128)(2,1)} %get-tuple-element.79), channel_id=1, source_target_pairs={{0,2},{8,10},{2,4},{10,12},{4,6},{12,14},{6,0},{14,8},{1,3},{9,11}... | collective-permute-start | bytes 884744 | tf_op jit(solution)/shard_map/ppermute | solution.py:486
  76.5 18.4 %collective-permute-start.20 = (bf16[48,3072]{1,0:T(8,128)(2,1)S(1)}, bf16[48,3072]{1,0:T(8,128)(2,1)}, u32[]{:S(2)}, u32[]{:S(2)}) collective-permute-start(bf16[48,3072]{1,0:T(8,128)(2,1)S(1)} %get-tuple-element.81), channel_id=1, source_target_pairs={{0,6},{8,14},{2,0},{10,8},{4,2},{12,10},{6,4},{14,12},{1,7},{9,15}... | collective-permute-start | bytes 884744 | tf_op jit(solution)/shard_map/ppermute | solution.py:486
  77.9 4.6 %collective-permute-start.16 = (bf16[4,144,128]{2,1,0:T(8,128)(2,1)S(1)}, bf16[4,144,128]{2,1,0:T(8,128)(2,1)S(1)}, u32[]{:S(2)}, u32[]{:S(2)}) collective-permute-start(bf16[4,144,128]{2,1,0:T(8,128)(2,1)S(1)} %bitcast.27), channel_id=1, source_target_pairs={{0,1},{1,0},{2,3},{3,2},{4,5},{5,4},{6,7},{7,6},{8,9},{9,8},{10,11... | collective-permute-start | bytes 442376 | tf_op jit(solution)/shard_map/ppermute | solution.py:481
  85.6 40.7 %all-to-all-start = ((bf16[64,144,128]{2,1,0:T(8,128)(2,1)}), bf16[64,144,128]{2,1,0:T(8,128)(2,1)S(1)}, u32[]{:S(2)}, u32[]{:S(2)}) async-start(bf16[64,144,128]{2,1,0:T(8,128)(2,1)} %pack.1), calls=%async_computation | async-start | bytes 4718592 | tf_op jit(solution)/shard_map/all_to_all | solution.py:541
  92.4 22.5 %collective-permute-start.17 = (bf16[48,3072]{1,0:T(8,128)(2,1)S(1)}, bf16[48,3072]{1,0:T(8,128)(2,1)S(1)}, u32[]{:S(2)}, u32[]{:S(2)}) collective-permute-start(bf16[48,3072]{1,0:T(8,128)(2,1)S(1)} %get-tuple-element.76), channel_id=1, source_target_pairs={{0,6},{8,14},{2,0},{10,8},{4,2},{12,10},{6,4},{14,12},{1,7},{9,15}... | collective-permute-start | bytes 884744 | tf_op jit(solution)/shard_map/ppermute | solution.py:486
  93.1 23.7 %collective-permute-start.18 = (bf16[48,3072]{1,0:T(8,128)(2,1)S(1)}, bf16[48,3072]{1,0:T(8,128)(2,1)}, u32[]{:S(2)}, u32[]{:S(2)}) collective-permute-start(bf16[48,3072]{1,0:T(8,128)(2,1)S(1)} %get-tuple-element.77), channel_id=1, source_target_pairs={{0,2},{8,10},{2,4},{10,12},{4,6},{12,14},{6,0},{14,8},{1,3},{9,11}... | collective-permute-start | bytes 884744 | tf_op jit(solution)/shard_map/ppermute | solution.py:486
  97.0 25.9 %collective-permute-start.21 = (bf16[48,3072]{1,0:T(8,128)(2,1)}, bf16[48,3072]{1,0:T(8,128)(2,1)S(1)}, u32[]{:S(2)}, u32[]{:S(2)}) collective-permute-start(bf16[48,3072]{1,0:T(8,128)(2,1)} %get-tuple-element.82), channel_id=1, source_target_pairs={{0,2},{8,10},{2,4},{10,12},{4,6},{12,14},{6,0},{14,8},{1,3},{9,11}... | collective-permute-start | bytes 884744 | tf_op jit(solution)/shard_map/ppermute | solution.py:486
  99.0 23.9 %collective-permute-start.22 = (bf16[48,3072]{1,0:T(8,128)(2,1)}, bf16[48,3072]{1,0:T(8,128)(2,1)}, u32[]{:S(2)}, u32[]{:S(2)}) collective-permute-start(bf16[48,3072]{1,0:T(8,128)(2,1)} %get-tuple-element.83), channel_id=1, source_target_pairs={{0,6},{8,14},{2,0},{10,8},{4,2},{12,10},{6,4},{14,12},{1,7},{9,15}... | collective-permute-start | bytes 884744 | tf_op jit(solution)/shard_map/ppermute | solution.py:486
  114.9 8.0 %copy-start.4 = (bf16[48,3072]{1,0:T(8,128)(2,1)}, bf16[48,3072]{1,0:T(8,128)(2,1)S(1)}, u32[]{:S(2)}) copy-start(bf16[48,3072]{1,0:T(8,128)(2,1)S(1)} %collective-permute-done.17.refs_2_) | copy-start | bytes 884740
  122.9 0.7 copy-start.5
